TPU v7x, 512 devices: a whole 4x8x8 slice. The times are simulated.
512 devices in a mesh: rep: 64 (over z, y), tp: 8 (over x, core).
Axes of the slice: x: 4, y: 8, z: 8, core: 2. Of those that a mesh axis runs over, the one named last changes fastest.
Arguments:
- kv_pool: bfloat16 [1024, 128, 1024], P('rep', None, 'tp'), may hold values from -6 to 6
- page_table: int32 [256, 4], P('rep'), may hold values from 0 to 15, as said below
- req_lengths: int32 [256], P('rep'), may hold values from 1 to 511, as said below
- leave_slot: int32 [64], P('rep'), may hold values from 0 to 3
- target_rep: int32 [64], P('rep'), may hold values from 0 to 63, as said below
- qkv_new: bfloat16 [256, 2560], P('rep', 'tp'), may hold values from -8.2 to 8.2
- residual_in: bfloat16 [256, 1536], P('rep'), may hold values from -6 to 6
- expert_ids: int32 [256, 4], P('rep'), may hold values from 0 to 7, all different within a row
- gate_weights: bfloat16 [256, 4], P('rep'), may hold values from 0.099609375 to 0.69921875
- norm_gain: float32 [1536], replicated, may hold values from 0.1 to 1.9
- out_proj: bfloat16 [1536, 1536], P('tp'), may hold values from -0.15625 to 0.15625
- expert_in: bfloat16 [8, 1536, 512], P('tp'), may hold values from -0.15625 to 0.15625
- expert_down: bfloat16 [8, 256, 1536], P('tp'), may hold values from -0.375 to 0.375
Outputs:
- hidden_out: bfloat16 [256, 1536], P('rep', 'tp')
- new_pages: bfloat16 [256, 128, 1024], P('rep', None, 'tp')
- arrived: bfloat16 [256, 128, 1024], P('rep', None, 'tp')
Inputs may be any that keep to these rules, and one draw needn't show every extreme that they name: `req_lengths`: in every draw the request that leaves some replica has length 511. `page_table`: the 4 rows of one replica hold each of its 16 pool pages once. `target_rep`: the targets form one cycle through all replicas: every replica receives exactly one request and none keeps its own; in every draw some replica sends to the replica half the axis of replicas away.
All inputs are finite; a program needn't handle non-finite values.
Results may differ from a plain program's by a relative error of at most 0.005.
Values may be sent and summed in bfloat16 or wider, within the bound.
A program may use at most 64 MiB of HBM per device.

v0:
```python
import math

import jax
import jax.numpy as jnp
from jax import lax
from jax.sharding import PartitionSpec as P

QH = 24
KVH = 8
HD = 64
FF = 256
PAGE = 128
MAXP = 4


def spread_slot(member, slot_mask):
    out_shape = (slot_mask.shape[0],) + (1,) * (member.ndim - 1)
    return jnp.where(slot_mask.reshape(out_shape), member, jnp.zeros((), member.dtype))


def fold_sum(member):
    if member.dtype == jnp.int32:
        return jnp.sum(member, axis=0, keepdims=True)
    return jnp.sum(member.astype(jnp.float32), axis=0, keepdims=True).astype(member.dtype)


def migrate(pages_out, row_data, resid_row, gate_row, int_row):
    slot_mask = jnp.arange(lax.axis_size("rep"), dtype=jnp.int32) == int_row[0, 1]
    landed = (
        lax.all_to_all(
            spread_slot(pages_out, slot_mask), "rep", split_axis=0, concat_axis=0, tiled=True
        ),
        lax.all_to_all(
            spread_slot(row_data, slot_mask), "rep", split_axis=0, concat_axis=0, tiled=True
        ),
        lax.all_to_all(
            spread_slot(resid_row, slot_mask), "rep", split_axis=0, concat_axis=0, tiled=True
        ),
        lax.all_to_all(
            spread_slot(gate_row, slot_mask), "rep", split_axis=0, concat_axis=0, tiled=True
        ),
        lax.all_to_all(
            spread_slot(int_row, slot_mask), "rep", split_axis=0, concat_axis=0, tiled=True
        ),
    )
    return tuple((fold_sum(member) for member in landed))


def write_token(cache_rows, new_kv, lengths):
    positions = jnp.arange(cache_rows.shape[1], dtype=jnp.int32)
    at_token = positions[None, :] == lengths[:, None]
    return jnp.where(at_token[:, :, None], new_kv[:, None, :], cache_rows)


def attend(queries, cache_rows, lengths):
    num_req, span_len, col_count = cache_rows.shape
    head_count = queries.shape[1]
    split_cache = cache_rows.reshape(num_req, span_len, head_count, 2, HD)
    scores = jnp.einsum(
        "rhgd,rlhd->rhgl", queries, split_cache[:, :, :, 0, :], preferred_element_type=jnp.float32
    ) * (1.0 / math.sqrt(HD))
    positions = jnp.arange(span_len, dtype=jnp.int32)
    visible = positions[None, :] <= lengths[:, None]
    scores = jnp.where(visible[:, None, None, :], scores, -jnp.inf)
    top_score = jnp.max(scores, axis=-1, keepdims=True)
    weights = jnp.exp(scores - top_score)
    probs = (weights / jnp.sum(weights, axis=-1, keepdims=True)).astype(jnp.bfloat16)
    attn_rows = jnp.einsum(
        "rhgl,rlhd->rhgd", probs, split_cache[:, :, :, 1, :], preferred_element_type=jnp.float32
    )
    return attn_rows.astype(jnp.bfloat16).reshape(num_req, -1)


def page_at(cache_rows, lengths):
    num_req, span_len, col_count = cache_rows.shape
    paged = cache_rows.reshape(num_req, span_len // PAGE, PAGE, col_count)
    return jnp.take_along_axis(paged, (lengths // PAGE)[:, None, None, None], axis=1)[:, 0]


def local(
    kv_pool,
    page_table,
    req_lengths,
    leave_slot,
    target_rep,
    qkv_new,
    residual_in,
    expert_ids,
    gate_weights,
    norm_gain,
    out_proj,
    expert_in,
    expert_down,
):
    num_req = residual_in.shape[0]
    group = QH // KVH
    head_local = kv_pool.shape[2] // (2 * HD)
    slot_hit = jnp.arange(num_req, dtype=jnp.int32) == leave_slot[0]
    own_cache = kv_pool[page_table].reshape(num_req, MAXP * PAGE, -1)
    int_row = jnp.concatenate(
        [req_lengths[leave_slot][:, None], target_rep[:, None], expert_ids[leave_slot]], axis=1
    )
    resid_row = residual_in[leave_slot]
    gate_row = gate_weights[leave_slot]
    pages_out = kv_pool[page_table[leave_slot[0]]][None]
    got_pages, got_qkv, got_resid, got_gates, got_ints = migrate(
        pages_out, qkv_new[leave_slot], resid_row, gate_row, int_row
    )
    cache_now = jnp.where(slot_hit[:, None, None], got_pages.reshape(1, MAXP * PAGE, -1), own_cache)
    qkv_now = jnp.where(slot_hit[:, None], got_qkv, qkv_new).reshape(
        num_req, head_local, group + 2, HD
    )
    len_now = jnp.where(slot_hit, got_ints[0, 0], req_lengths)
    cache_now = write_token(cache_now, qkv_now[:, :, group:, :].reshape(num_req, -1), len_now)
    attn_rows = attend(qkv_now[:, :, :group, :], cache_now, len_now)
    new_pages = page_at(cache_now, len_now)
    arrived_pages = cache_now[leave_slot[0]].reshape(MAXP, PAGE, -1)
    resid_now = jnp.where(slot_hit[:, None], got_resid, residual_in)
    gates_now = jnp.where(slot_hit[:, None], got_gates, gate_weights)
    ids_now = jnp.where(slot_hit[:, None], got_ints[:, 2:], expert_ids)
    head_part = jnp.dot(attn_rows, out_proj, preferred_element_type=jnp.float32)
    tp_index = lax.axis_index("tp")
    col_count = norm_gain.shape[0] // lax.axis_size("tp")
    stream_full = resid_now.astype(jnp.float32) + lax.psum(head_part, "tp")
    mean_sq = jnp.mean(stream_full * stream_full, axis=1, keepdims=True)
    normed = (stream_full * lax.rsqrt(mean_sq + 1e-05) * norm_gain).astype(jnp.bfloat16)
    stream_share = lax.dynamic_slice_in_dim(stream_full, tp_index * col_count, col_count, 1)
    expert_local = expert_in.shape[0]
    expert_number = tp_index * expert_local + 0
    route_share = jnp.sum(
        jnp.where(ids_now == expert_number, gates_now.astype(jnp.float32), 0.0), axis=1
    )
    up_both = jnp.dot(normed, expert_in[0], preferred_element_type=jnp.float32)
    acted = (jax.nn.silu(up_both[:, :FF]) * up_both[:, FF:]).astype(jnp.bfloat16)
    expert_total = route_share[:, None] * jnp.dot(
        acted, expert_down[0], preferred_element_type=jnp.float32
    )
    moe_share = lax.psum_scatter(expert_total, "tp", scatter_dimension=1, tiled=True)
    hidden_out = (stream_share + moe_share).astype(jnp.bfloat16)
    return (hidden_out, new_pages, arrived_pages)


def solution(mesh):
    return jax.shard_map(
        local,
        mesh=mesh,
        in_specs=(
            P("rep", None, "tp"),
            P("rep", None),
            P("rep"),
            P("rep"),
            P("rep"),
            P("rep", "tp"),
            P("rep", None),
            P("rep", None),
            P("rep", None),
            P(),
            P("tp", None),
            P("tp", None, None),
            P("tp", None, None),
        ),
        out_specs=(P("rep", "tp"), P("rep", None, "tp"), P("rep", None, "tp")),
        check_vma=False,
    )
```

profile of v0, /device:TPU:1, one launch (start us, length us, event | category | flops | bytes accessed | tf_op | source)
XLA Modules:
  0.0 460.2 jit_solution(5060445487903094574)
XLA Ops:
  10.1 17.1 %all-to-all-start.4 = ((bf16[64,1,4]{2,1,0:T(2,128)(2,1)}), bf16[64,1,4]{2,1,0:T(2,128)(2,1)S(1)}, u32[]{:S(2)}, u32[]{:S(2)}) async-start(bf16[64,1,4]{2,1,0:T(2,128)(2,1)} %broadcast_select_fusion.4), calls=%async_computation.4 | async-start | bytes 65536 | tf_op jit(solution)/shard_map/all_to_all | solution.py:39
  27.2 1.3 dynamic-slice.15
  32.7 5.3 %all-to-all-done.4 = bf16[64,1,4]{2,1,0:T(2,128)(2,1)S(1)} async-done(((bf16[64,1,4]{2,1,0:T(2,128)(2,1)}), bf16[64,1,4]{2,1,0:T(2,128)(2,1)S(1)}, u32[]{:S(2)}, u32[]{:S(2)}) %all-to-all-start.4) | async-done | bytes 544 | tf_op jit(solution)/shard_map/all_to_all | solution.py:39
  38.0 6.9 %all-to-all-start.1 = ((s32[64,1,6]{2,1,0:T(1,128)}), s32[64,1,6]{2,1,0:T(1,128)S(1)}, u32[]{:S(2)}, u32[]{:S(2)}) async-start(s32[64,1,6]{2,1,0:T(1,128)} %broadcast_select_fusion.5), calls=%async_computation.1 | async-start | bytes 65536 | tf_op jit(solution)/shard_map/all_to_all | solution.py:42
  47.7 1.8 reduce.17
  50.3 5.4 %all-to-all-done.1 = s32[64,1,6]{2,1,0:T(1,128)S(1)} async-done(((s32[64,1,6]{2,1,0:T(1,128)}), s32[64,1,6]{2,1,0:T(1,128)S(1)}, u32[]{:S(2)}, u32[]{:S(2)}) %all-to-all-start.1) | async-done | bytes 1568 | tf_op jit(solution)/shard_map/all_to_all | solution.py:42
  55.6 6.8 %all-to-all-start.2 = ((bf16[64,2,160]{2,1,0:T(2,128)(2,1)}), bf16[64,2,160]{2,1,0:T(2,128)(2,1)S(1)}, u32[]{:S(2)}, u32[]{:S(2)}) async-start(bf16[64,2,160]{2,1,0:T(2,128)(2,1)} %reshape.552), calls=%async_computation.2 | async-start | bytes 131072 | tf_op jit(solution)/shard_map/all_to_all | solution.py:33
  62.4 1.6 gather_fusion
  64.0 9.4 %all-to-all-done.2 = bf16[64,2,160]{2,1,0:T(2,128)(2,1)S(1)} async-done(((bf16[64,2,160]{2,1,0:T(2,128)(2,1)}), bf16[64,2,160]{2,1,0:T(2,128)(2,1)S(1)}, u32[]{:S(2)}, u32[]{:S(2)}) %all-to-all-start.2) | async-done | bytes 40992 | tf_op jit(solution)/shard_map/all_to_all | solution.py:33
  73.5 4.6 %all-to-all-start = ((bf16[64,2,768]{2,1,0:T(2,128)(2,1)}), bf16[64,2,768]{2,1,0:T(2,128)(2,1)S(1)}, u32[]{:S(2)}, u32[]{:S(2)}) async-start(bf16[64,2,768]{2,1,0:T(2,128)(2,1)} %reshape.554), calls=%async_computation | async-start | bytes 393216 | tf_op jit(solution)/shard_map/all_to_all | solution.py:36
  78.1 3.8 broadcast_select_fusion
  82.0 8.2 %all-to-all-done = bf16[64,2,768]{2,1,0:T(2,128)(2,1)S(1)} async-done(((bf16[64,2,768]{2,1,0:T(2,128)(2,1)}), bf16[64,2,768]{2,1,0:T(2,128)(2,1)S(1)}, u32[]{:S(2)}, u32[]{:S(2)}) %all-to-all-start) | async-done | bytes 196640 | tf_op jit(solution)/shard_map/all_to_all | solution.py:36
  90.1 5.8 %all-to-all-start.3 = ((bf16[64,4,128,128]{3,2,1,0:T(8,128)(2,1)}), bf16[64,4,128,128]{3,2,1,0:T(8,128)(2,1)}, u32[]{:S(2)}, u32[]{:S(2)}) async-start(bf16[64,4,128,128]{3,2,1,0:T(8,128)(2,1)} %broadcast_select_fusion), calls=%async_computation.3 | async-start | bytes 16777216 | tf_op jit(solution)/shard_map/all_to_all | solution.py:30
  97.3 1.8 copy.49
  106.6 234.8 %all-to-all-done.3 = bf16[64,4,128,128]{3,2,1,0:T(8,128)(2,1)} async-done(((bf16[64,4,128,128]{3,2,1,0:T(8,128)(2,1)}), bf16[64,4,128,128]{3,2,1,0:T(8,128)(2,1)}, u32[]{:S(2)}, u32[]{:S(2)}) %all-to-all-start.3) | async-done | bytes 8388640 | tf_op jit(solution)/shard_map/all_to_all | solution.py:30
  341.3 5.1 %reduce.11 = bf16[4,128,128]{2,1,0:T(8,128)(2,1)S(1)} reduce(bf16[64,4,128,128]{3,2,1,0:T(8,128)(2,1)} %all-to-all-done.3, bf16[]{:T(256)} %constant.25.clone.1), dimensions={0}, to_apply=%region_3.4.clone | reduce | flops 4128768 | bytes 8519682 | tf_op jit(solution)/shard_map/reduce_sum | solution.py:24
  347.2 1.6 convert_element_type.67
  348.9 1.8 select_select_fusion.1
  353.3 1.3 fusion.22
  354.5 25.4 %psum.7 = f32[4,1536]{1,0:T(4,128)S(1)} all-reduce(f32[4,1536]{1,0:T(4,128)S(1)} %fusion.22), channel_id=1, replica_groups=mesh['rep'=64,'tp'=8] {'tp'}, use_global_device_ids=true, to_apply=%region_6.7 | all-reduce | flops 6144 | bytes 49152 | tf_op jit(solution)/shard_map/psum | solution.py:124
  385.7 2.2 fusion.7
  387.9 1.3 broadcast_select_fusion.3
  389.2 61.8 %reduce-scatter.4.cloned.1.call-done = f32[192,4]{1,0:T(8,128)} async-done(((f32[1536,4]{1,0:T(8,128)}), f32[192,4]{1,0:T(8,128)}) %reduce-scatter.4.cloned.1.call-update) | async-done | bytes 3088
  452.0 1.4 add_convert_fusion
  (88 shorter events, 28.0 us)
Async XLA Ops:
  7.2 373.7 %copy-start = (bf16[1,1536,512]{2,1,0:T(8,128)(2,1)S(1)}, bf16[1,1536,512]{2,1,0:T(8,128)(2,1)}, u32[]{:S(2)}) copy-start(bf16[1,1536,512]{2,1,0:T(8,128)(2,1)} %param.24) | copy-start | bytes 4718596
  10.1 27.9 %all-to-all-start.4 = ((bf16[64,1,4]{2,1,0:T(2,128)(2,1)}), bf16[64,1,4]{2,1,0:T(2,128)(2,1)S(1)}, u32[]{:S(2)}, u32[]{:S(2)}) async-start(bf16[64,1,4]{2,1,0:T(2,128)(2,1)} %broadcast_select_fusion.4), calls=%async_computation.4 | async-start | bytes 65536 | tf_op jit(solution)/shard_map/all_to_all | solution.py:39
  38.0 17.7 %all-to-all-start.1 = ((s32[64,1,6]{2,1,0:T(1,128)}), s32[64,1,6]{2,1,0:T(1,128)S(1)}, u32[]{:S(2)}, u32[]{:S(2)}) async-start(s32[64,1,6]{2,1,0:T(1,128)} %broadcast_select_fusion.5), calls=%async_computation.1 | async-start | bytes 65536 | tf_op jit(solution)/shard_map/all_to_all | solution.py:42
  55.6 17.9 %all-to-all-start.2 = ((bf16[64,2,160]{2,1,0:T(2,128)(2,1)}), bf16[64,2,160]{2,1,0:T(2,128)(2,1)S(1)}, u32[]{:S(2)}, u32[]{:S(2)}) async-start(bf16[64,2,160]{2,1,0:T(2,128)(2,1)} %reshape.552), calls=%async_computation.2 | async-start | bytes 131072 | tf_op jit(solution)/shard_map/all_to_all | solution.py:33
  73.5 16.6 %all-to-all-start = ((bf16[64,2,768]{2,1,0:T(2,128)(2,1)}), bf16[64,2,768]{2,1,0:T(2,128)(2,1)S(1)}, u32[]{:S(2)}, u32[]{:S(2)}) async-start(bf16[64,2,768]{2,1,0:T(2,128)(2,1)} %reshape.554), calls=%async_computation | async-start | bytes 393216 | tf_op jit(solution)/shard_map/all_to_all | solution.py:36
  82.0 14.2 %copy-start.10 = (s32[4,4]{1,0:T(4,128)S(1)}, s32[4,4]{1,0:T(4,128)}, u32[]{:S(2)}) copy-start(s32[4,4]{1,0:T(4,128)} %param.14) | copy-start | bytes 196
  82.0 14.3 %copy-start.2 = (bf16[16,128,128]{2,1,0:T(8,128)(2,1)S(1)}, bf16[16,128,128]{2,1,0:T(8,128)(2,1)}, u32[]{:S(2)}) copy-start(bf16[16,128,128]{2,1,0:T(8,128)(2,1)} %param.13) | copy-start | bytes 1572868
  82.0 18.1 %copy-start.13 = (s32[4]{0:T(128)S(1)}, s32[4]{0:T(128)}, u32[]{:S(2)}) copy-start(s32[4]{0:T(128)} %param.15) | copy-start | bytes 52
  82.0 20.0 %copy-start.11 = (s32[4,4]{1,0:T(4,128)S(1)}, s32[4,4]{1,0:T(4,128)}, u32[]{:S(2)}) copy-start(s32[4,4]{1,0:T(4,128)} %param.20) | copy-start | bytes 196
  82.0 20.0 %copy-start.12 = (bf16[4,4]{1,0:T(4,128)(2,1)S(1)}, bf16[4,4]{1,0:T(4,128)(2,1)}, u32[]{:S(2)}) copy-start(bf16[4,4]{1,0:T(4,128)(2,1)} %param.21) | copy-start | bytes 100
  82.0 22.1 %copy-start.8 = (bf16[4,320]{1,0:T(4,128)(2,1)S(1)}, bf16[4,320]{1,0:T(4,128)(2,1)}, u32[]{:S(2)}) copy-start(bf16[4,320]{1,0:T(4,128)(2,1)} %param.18) | copy-start | bytes 7684
  90.1 251.2 %all-to-all-start.3 = ((bf16[64,4,128,128]{3,2,1,0:T(8,128)(2,1)}), bf16[64,4,128,128]{3,2,1,0:T(8,128)(2,1)}, u32[]{:S(2)}, u32[]{:S(2)}) async-start(bf16[64,4,128,128]{3,2,1,0:T(8,128)(2,1)} %broadcast_select_fusion), calls=%async_computation.3 | async-start | bytes 16777216 | tf_op jit(solution)/shard_map/all_to_all | solution.py:30
  95.9 355.1 %reduce-scatter.4.cloned.1.call-start = ((), (), s32[]{:S(2)}) async-start(), calls=%async_computation.6 | async-start | bytes 884736
  96.9 283.0 %copy-start.5 = (bf16[4,1536]{1,0:T(4,128)(2,1)S(1)}, bf16[4,1536]{1,0:T(4,128)(2,1)}, u32[]{:S(2)}) copy-start(bf16[4,1536]{1,0:T(4,128)(2,1)} %param.19) | copy-start | bytes 36868
  99.2 249.7 %copy-start.1 = (bf16[4,512,1,2,64]{1,4,0,3,2:T(8,128)(2,1)S(1)}, bf16[4,512,1,2,64]{1,4,0,3,2:T(8,128)(2,1)}, u32[]{:S(2)}) copy-start(bf16[4,512,1,2,64]{1,4,0,3,2:T(8,128)(2,1)} %copy.49) | copy-start | bytes 1572868
  99.2 7.4 %copy-start.6 = (pred[4]{0:T(512)(128)(4,1)}, pred[4]{0:T(512)(128)(4,1)S(1)}, u32[]{:S(2)}) copy-start(pred[4]{0:T(512)(128)(4,1)S(1)} %iota_compare_fusion.3) | copy-start | bytes 16
  104.3 2.3 copy-start.7
  104.9 1.6 copy-start.9
  106.6 275.3 %copy-start.3 = (bf16[1,256,1536]{2,1,0:T(8,128)(2,1)S(1)}, bf16[1,256,1536]{2,1,0:T(8,128)(2,1)}, u32[]{:S(2)}) copy-start(bf16[1,256,1536]{2,1,0:T(8,128)(2,1)} %param.25) | copy-start | bytes 2359300
  380.8 3.1 copy-start.4
Sparse Core Ops, SparseCore 0:
  384.1 66.8 reduce-scatter.3
where the time goes:
time: 462 us; the launch traced here: 460 us
  waiting for transfers between devices  325 us (70%)
  starting transfers between devices  41.4 us (9%)
  other arithmetic  28.4 us (6%)
  blocking collectives  25.4 us (5%)
  local copies, waits for them, and re-layouts  19 us (4%)
  between operations  15.7 us (3%)
  matrix products  5.43 us (1%)
    all_to_all x1, waiting for transfers between devices, migrate(): lax.all_to_all(spread_slot(pages_out, slot_mask), 'rep', split_axis=0, co...  235 us
    unnamed x2, waiting for transfers between devices  61.8 us
    psum x1, blocking collectives, local(): stream_full = resid_now.astype(jnp.float32) + lax.psum(head_part, 'tp')  25.4 us
    all_to_all x1, starting transfers between devices, migrate(): lax.all_to_all(spread_slot(gate_row, slot_mask), 'rep', split_axis=0, con...  17.1 us
    all_to_all x1, waiting for transfers between devices, migrate(): lax.all_to_all(spread_slot(row_data, slot_mask), 'rep', split_axis=0, con...  9.44 us
  transfers between devices with their start and end apart: 6, of which 6 were waited for; matrix products, arithmetic and copies ran while one was open for 7% of the time, Pallas kernels for 0%

commit v1 on v0

v1 whole, which is shorter than its diff:
```python
import functools
import math

import jax
import jax.numpy as jnp
from jax import lax
from jax.experimental import pallas as pl
from jax.experimental.pallas import tpu as pltpu
from jax.sharding import PartitionSpec as P

HD = 64
PAGE = 128
MAXP = 4
REQ = 4
GROUP = 3
LANES = 128
TILE = 16
PG = PAGE // TILE
F32 = jnp.float32
BF16 = jnp.bfloat16
MESH = pl.DeviceIdType.MESH


def dot(a, b):
    return jnp.dot(a, b, preferred_element_type=F32)


def kernel(
    nz,
    ny,
    ntp,
    pt_ref,
    len_ref,
    leave_ref,
    target_ref,
    qkv_ref,
    res_ref,
    ids_ref,
    gate_ref,
    gain_ref,
    pool_hbm,
    wo_hbm,
    win_hbm,
    wd_hbm,
    hid_out,
    newp_out,
    arr_out,
    pool,
    wo,
    win,
    wd,
    qs,
    cache,
    first_a,
    first_b,
    send_a,
    send_b,
    last_a,
    last_b,
    parts,
    stream8,
    share_out,
    share_in,
    row_y,
    row_send,
    row_z,
    load_sem,
    send_sem,
    recv_sem,
):
    rep = lax.axis_index("rep")
    tp = lax.axis_index("tp")
    z = lax.div(rep, ny)
    y = lax.rem(rep, ny)

    def on_y(step):
        return {"rep": z * ny + lax.rem(y + step, ny)}

    def on_z(step):
        return {"rep": lax.rem(z + step, nz) * ny + y}

    def on_tp(step):
        return {"tp": lax.rem(tp + step, ntp)}

    loads = [
        pltpu.make_async_copy(pool_hbm, pool, load_sem.at[0]),
        pltpu.make_async_copy(wo_hbm, wo, load_sem.at[1]),
        pltpu.make_async_copy(win_hbm.at[0], win, load_sem.at[2]),
        pltpu.make_async_copy(wd_hbm.at[0], wd, load_sem.at[3]),
    ]
    for copy in loads:
        copy.start()

    barrier = pltpu.get_barrier_semaphore()
    for peer, count in ((on_y, ny), (on_z, nz), (on_tp, ntp)):
        for step in range(1, count):
            pl.semaphore_signal(barrier, inc=1, device_id=peer(step), device_id_type=MESH)

    def push(kind, step, src, dst, peer):
        copy = pltpu.make_async_remote_copy(
            src_ref=src,
            dst_ref=dst,
            send_sem=send_sem.at[kind, step],
            recv_sem=recv_sem.at[kind, step],
            device_id=peer(step),
            device_id_type=MESH,
        )
        copy.start()
        return copy

    leave = leave_ref[0]
    target = target_ref[0]
    low = lax.broadcasted_iota(jnp.int32, (8, LANES), 1) < HD
    qs[...] = jnp.zeros_like(qs)
    qs[0:REQ, 0 : (GROUP + 2) * HD] = qkv_ref[...].astype(F32)
    qkv_a, qkv_b, qkv_c = qs[:, 0:128], qs[:, 128:256], qs[:, 256:384]
    zero8 = jnp.zeros((8, LANES), F32)
    queries = jnp.concatenate(
        [
            jnp.where(low, qkv_a, zero8),
            jnp.where(low, pltpu.roll(qkv_a, HD, 1), zero8),
            jnp.where(low, qkv_b, zero8),
        ],
        axis=0,
    ).astype(BF16)
    fresh = jnp.where(low, pltpu.roll(qkv_b, HD, 1), pltpu.roll(qkv_c, HD, 1))

    loads[0].wait()
    row_in_page = lax.broadcasted_iota(jnp.int32, (PAGE, LANES), 0)
    for r in range(REQ):
        new_row = fresh[r : r + 1, :]
        for p in range(MAXP):
            page = pool[pt_ref[r, p]].astype(F32)
            at_token = row_in_page == len_ref[r] - p * PAGE
            cache[r, p] = jnp.where(at_token, new_row, page).astype(BF16)

    header = jnp.full((TILE, LANES), target, jnp.int32).astype(F32).astype(BF16)
    for buf, p0 in ((first_a, 0), (first_b, 2)):
        for i in range(2):
            buf[0, i * PG : (i + 1) * PG] = cache[leave, p0 + i].reshape(PG, TILE, LANES)
        buf[0, 2 * PG] = header

    pl.semaphore_wait(barrier, ny - 1 + nz - 1 + ntp - 1)
    gather_a = [push(0, d, first_a.at[0], first_a.at[d], on_y) for d in range(1, ny)]
    gather_b = [push(1, d, first_b.at[0], first_b.at[d], on_z) for d in range(1, nz)]

    span = MAXP * PAGE
    row_req = lax.broadcasted_iota(jnp.int32, (GROUP * 8, span), 0) & 7
    position = lax.broadcasted_iota(jnp.int32, (GROUP * 8, span), 1)
    scores = jnp.zeros((GROUP * 8, span), F32)
    limit = jnp.zeros((GROUP * 8, span), jnp.int32)
    for r in range(REQ):
        rows = cache[r].reshape(span, LANES)
        one = lax.dot_general(
            queries, rows, (((1,), (1,)), ((), ())), preferred_element_type=F32
        )
        scores = jnp.where(row_req == r, one, scores)
        limit = jnp.where(row_req == r, len_ref[r], limit)
    scores = jnp.where(position <= limit, scores * (1.0 / math.sqrt(HD)), -jnp.inf)
    weights = jnp.exp(scores - jnp.max(scores, axis=1, keepdims=True))
    probs = weights / jnp.sum(weights, axis=1, keepdims=True)
    attn = jnp.zeros((GROUP * 8, LANES), F32)
    for r in range(REQ):
        rows = cache[r].reshape(span, LANES)
        attn = attn + dot(jnp.where(row_req == r, probs, 0.0).astype(BF16), rows)
    heads01 = jnp.where(low, pltpu.roll(attn[0:8], HD, 1), attn[8:16]).astype(BF16)
    head2 = pltpu.roll(attn[16:24], HD, 1)[:, 0:HD].astype(BF16)
    loads[1].wait()
    part = dot(heads01, wo[0:LANES, :]) + dot(head2, wo[LANES : LANES + HD, :])
    parts[0] = part[0:REQ]
    sum_heads = [push(2, d, parts.at[0], parts.at[d], on_tp) for d in range(1, ntp)]

    share = jnp.sum(
        jnp.where(ids_ref[...] == tp, gate_ref[...].astype(F32), 0.0), axis=1, keepdims=True
    )
    total = res_ref[...].astype(F32) + parts[0]
    for d in range(1, ntp):
        sum_heads[d - 1].wait_recv()
        total = total + parts[d]
    stream8[...] = jnp.zeros_like(stream8)
    stream8[0:REQ, :] = total
    stream = stream8[...]
    mean_sq = jnp.mean(stream * stream, axis=1, keepdims=True)
    normed = (stream * lax.rsqrt(mean_sq + 1e-05) * gain_ref[...]).astype(BF16)
    loads[2].wait()
    up = dot(normed, win[...])
    half = up.shape[1] // 2
    gate, lift = up[:, 0:half], up[:, half:]
    acted = (gate * (1.0 / (1.0 + jnp.exp(-gate))) * lift).astype(BF16)
    loads[3].wait()
    down = dot(acted, wd[...])
    stream8[0:REQ, :] = down[0:REQ] * share + jnp.where(tp == 0, 1.0, 0.0) * total
    cols = stream8.shape[1] // ntp
    for t in range(ntp):
        start = t * cols // LANES * LANES
        window = stream8[:, start : start + 2 * LANES]
        if t * cols != start:
            window = jnp.concatenate(
                [
                    jnp.where(
                        low,
                        pltpu.roll(window[:, 0:LANES], HD, 1),
                        pltpu.roll(window[:, LANES:], HD, 1),
                    ),
                    pltpu.roll(window[:, LANES:], HD, 1),
                ],
                axis=1,
            )
        share_out[t] = window
    sum_experts = [
        push(3, d, share_out.at[lax.rem(tp + d, ntp)], share_in.at[d], on_tp)
        for d in range(1, ntp)
    ]

    def forward(first, send, last, waits, kind, peer, count, number_of):
        for copy in waits:
            copy.wait_recv()
        heads = [first[d, 2 * PG].astype(F32) for d in range(len(waits) + 1)]
        sent = []
        for e in range(count):
            wanted = number_of(e).astype(F32)
            packet = jnp.zeros((2 * PG, TILE, LANES), BF16)
            for d, head in enumerate(heads):
                mine = jnp.where(head == wanted, 1.0, 0.0).astype(BF16)
                packet = packet + first[d, 0 : 2 * PG] * mine[None]
            if e == 0:
                last[0] = packet
            else:
                send[e] = packet
                sent.append(push(kind, e, send.at[e], last.at[e], peer))
        return sent

    def number_z(e):
        return lax.rem(z + e, nz) * ny + y

    def number_y(e):
        return z * ny + lax.rem(y + e, ny)

    scatter_a = forward(first_a, send_a, last_a, gather_a, 4, on_z, nz, number_z)
    scatter_b = forward(first_b, send_b, last_b, gather_b, 5, on_y, ny, number_y)

    hidden = share_out[tp]
    for d in range(1, ntp):
        sum_experts[d - 1].wait_recv()
        hidden = hidden + share_in[d]
    row8 = lax.broadcasted_iota(jnp.int32, hidden.shape, 0)
    leaving = jnp.sum(jnp.where(row8 == leave, hidden, 0.0), axis=0, keepdims=True)
    page_no = lax.shift_right_logical(len_ref[leave], 7)
    row_y[0] = jnp.where(
        row8 == 0,
        leaving,
        jnp.where(row8 == 1, target, jnp.where(row8 == 2, page_no, 0)).astype(F32),
    )
    rows_y = [push(6, d, row_y.at[0], row_y.at[d], on_y) for d in range(1, ny)]
    for copy in rows_y:
        copy.wait_recv()
    rows_z = []
    for e in range(nz):
        wanted = number_z(e).astype(F32)
        message = jnp.zeros(hidden.shape, F32)
        for d in range(ny):
            one = row_y[d]
            message = message + jnp.where(one[1:2, :] == wanted, 1.0, 0.0) * one
        if e == 0:
            row_z[0] = message
        else:
            row_send[e] = message
            rows_z.append(push(7, e, row_send.at[e], row_z.at[e], on_z))
    message = row_z[0]
    for e in range(1, nz):
        rows_z[e - 1].wait_recv()
        message = message + row_z[e]
    hidden = jnp.where(row8 == leave, message[0:1, :], hidden)
    hid_out[...] = hidden[0:REQ, 0:cols].astype(BF16)

    came_page = jnp.broadcast_to(message[2:3, 0:LANES], (TILE, LANES))
    moved = jnp.zeros((PG, TILE, LANES), BF16)
    for last, waits, p0 in ((last_a, scatter_a, 0), (last_b, scatter_b, 2)):
        came = last[0]
        for e in range(1, len(waits) + 1):
            waits[e - 1].wait_recv()
            came = came + last[e]
        for i in range(2):
            page = came[i * PG : (i + 1) * PG]
            arr_out[p0 + i] = page.reshape(PAGE, LANES)
            mine = jnp.where(came_page == float(p0 + i), 1.0, 0.0).astype(BF16)
            moved = moved + page * mine[None]
    for r in range(REQ):
        kept = jnp.full((TILE, LANES), jnp.where(leave == r, 0.0, 1.0), F32)
        stays = cache[r, lax.shift_right_logical(len_ref[r], 7)].reshape(PG, TILE, LANES)
        page = stays * kept.astype(BF16)[None] + moved * (1.0 - kept).astype(BF16)[None]
        newp_out[r] = page.reshape(PAGE, LANES)

    for copies in (
        gather_a,
        gather_b,
        sum_heads,
        sum_experts,
        scatter_a,
        scatter_b,
        rows_y,
        rows_z,
    ):
        for copy in copies:
            copy.wait_send()


def local(
    nz,
    ny,
    ntp,
    kv_pool,
    page_table,
    req_lengths,
    leave_slot,
    target_rep,
    qkv_new,
    residual_in,
    expert_ids,
    gate_weights,
    norm_gain,
    out_proj,
    expert_in,
    expert_down,
):
    width = residual_in.shape[1]
    cols = width // ntp
    most = max(nz, ny, ntp)
    smem = pl.BlockSpec(memory_space=pltpu.SMEM)
    vmem = pl.BlockSpec(memory_space=pltpu.VMEM)
    hbm = pl.BlockSpec(memory_space=pl.ANY)
    return pl.pallas_call(
        functools.partial(kernel, nz, ny, ntp),
        out_shape=(
            jax.ShapeDtypeStruct((REQ, cols), BF16),
            jax.ShapeDtypeStruct((REQ, PAGE, LANES), BF16),
            jax.ShapeDtypeStruct((MAXP, PAGE, LANES), BF16),
        ),
        in_specs=[smem] * 4 + [vmem] * 5 + [hbm] * 4,
        out_specs=(vmem, vmem, vmem),
        scratch_shapes=[
            pltpu.VMEM(kv_pool.shape, BF16),
            pltpu.VMEM(out_proj.shape, BF16),
            pltpu.VMEM(expert_in.shape[1:], BF16),
            pltpu.VMEM(expert_down.shape[1:], BF16),
            pltpu.VMEM((8, 3 * LANES), F32),
            pltpu.VMEM((REQ, MAXP, PAGE, LANES), BF16),
            pltpu.VMEM((ny, 2 * PG + 1, TILE, LANES), BF16),
            pltpu.VMEM((nz, 2 * PG + 1, TILE, LANES), BF16),
            pltpu.VMEM((nz, 2 * PG, TILE, LANES), BF16),
            pltpu.VMEM((ny, 2 * PG, TILE, LANES), BF16),
            pltpu.VMEM((nz, 2 * PG, TILE, LANES), BF16),
            pltpu.VMEM((ny, 2 * PG, TILE, LANES), BF16),
            pltpu.VMEM((ntp, REQ, width), F32),
            pltpu.VMEM((8, width), F32),
            pltpu.VMEM((ntp, 8, 2 * LANES), F32),
            pltpu.VMEM((ntp, 8, 2 * LANES), F32),
            pltpu.VMEM((ny, 8, 2 * LANES), F32),
            pltpu.VMEM((nz, 8, 2 * LANES), F32),
            pltpu.VMEM((nz, 8, 2 * LANES), F32),
            pltpu.SemaphoreType.DMA((4,)),
            pltpu.SemaphoreType.DMA((8, most)),
            pltpu.SemaphoreType.DMA((8, most)),
        ],
        compiler_params=pltpu.CompilerParams(
            collective_id=0, has_side_effects=True, vmem_limit_bytes=32 << 20
        ),
    )(
        page_table,
        req_lengths,
        leave_slot,
        target_rep,
        qkv_new,
        residual_in,
        expert_ids,
        gate_weights,
        norm_gain[None, :],
        kv_pool,
        out_proj,
        expert_in,
        expert_down,
    )


def solution(mesh):
    nrep, ntp = mesh.shape["rep"], mesh.shape["tp"]
    ny = math.isqrt(nrep)
    return jax.shard_map(
        functools.partial(local, nrep // ny, ny, ntp),
        mesh=mesh,
        in_specs=(
            P("rep", None, "tp"),
            P("rep", None),
            P("rep"),
            P("rep"),
            P("rep"),
            P("rep", "tp"),
            P("rep", None),
            P("rep", None),
            P("rep", None),
            P(),
            P("tp", None),
            P("tp", None, None),
            P("tp", None, None),
        ),
        out_specs=(P("rep", "tp"), P("rep", None, "tp"), P("rep", None, "tp")),
        check_vma=False,
    )
```

time: 462 us -> 64.8 us (0.14)
  the two profiles are of different devices: /device:TPU:1 before, /device:TPU:2 now
where the time goes in v1:
time: 64.8 us; the launch traced here: 64.3 us
  Pallas kernels  51 us (79%)
  local copies, waits for them, and re-layouts  11.3 us (17%)
  between operations  1.94 us (3%)
    pallas_call x1, Pallas kernels, local(): pl.pallas_call(functools.partial(kernel, nz, ny, ntp), out_shape=(jax.Sha...  51 us
    unnamed x23, local copies, waits for them, and re-layouts  10.6 us

profile of v1, /device:TPU:2, one launch (start us, length us, event | category | flops | bytes accessed | tf_op | source)
XLA Modules:
  0.0 64.3 jit_solution(3862333247799910318)
XLA Ops:
  1.9 0.7 %broadcast_in_dim.3.gain_ref = f32[1,1536]{1,0:T(1,128)S(1)} reshape(f32[1536]{0:T(1024)} %param.22) | data formatting | bytes 12288 | tf_op jit(solution)/shard_map/broadcast_in_dim | solution.py:377
  2.6 0.0 copy-start
  2.6 1.4 %copy-done = bf16[1,1536,512]{2,1,0:T(8,128)(2,1)S(1)} copy-done((bf16[1,1536,512]{2,1,0:T(8,128)(2,1)S(1)}, bf16[1,1536,512]{2,1,0:T(8,128)(2,1)}, u32[]{:S(2)}) %copy-start) | copy-done | bytes 1572888
  4.0 0.0 copy-start.1
  4.0 1.1 %copy-done.1 = bf16[1,256,1536]{2,1,0:T(8,128)(2,1)S(1)} copy-done((bf16[1,256,1536]{2,1,0:T(8,128)(2,1)S(1)}, bf16[1,256,1536]{2,1,0:T(8,128)(2,1)}, u32[]{:S(2)}) %copy-start.1) | copy-done | bytes 786456
  5.2 0.0 copy-start.2
  5.2 1.1 %copy-done.2 = bf16[192,1536]{1,0:T(8,128)(2,1)S(1)} copy-done((bf16[192,1536]{1,0:T(8,128)(2,1)S(1)}, bf16[192,1536]{1,0:T(8,128)(2,1)}, u32[]{:S(2)}) %copy-start.2) | copy-done | bytes 589848
  6.2 0.0 copy-start.3
  6.2 1.0 %copy-done.3 = bf16[16,128,128]{2,1,0:T(8,128)(2,1)S(1)} copy-done((bf16[16,128,128]{2,1,0:T(8,128)(2,1)S(1)}, bf16[16,128,128]{2,1,0:T(8,128)(2,1)}, u32[]{:S(2)}) %copy-start.3) | copy-done | bytes 524312
  7.3 0.0 copy-start.4
  7.3 0.7 %copy-done.4 = bf16[4,1536]{1,0:T(4,128)(2,1)S(1)} copy-done((bf16[4,1536]{1,0:T(4,128)(2,1)S(1)}, bf16[4,1536]{1,0:T(4,128)(2,1)}, u32[]{:S(2)}) %copy-start.4) | copy-done | bytes 12312
  8.0 0.0 copy-start.5
  8.0 0.7 %copy-done.5 = bf16[4,320]{1,0:T(4,128)(2,1)S(1)} copy-done((bf16[4,320]{1,0:T(4,128)(2,1)S(1)}, bf16[4,320]{1,0:T(4,128)(2,1)}, u32[]{:S(2)}) %copy-start.5) | copy-done | bytes 2584
  8.7 0.0 copy-start.6
  8.7 0.7 %copy-done.6 = s32[4,4]{1,0:T(4,128)S(1)} copy-done((s32[4,4]{1,0:T(4,128)S(1)}, s32[4,4]{1,0:T(4,128)}, u32[]{:S(2)}) %copy-start.6) | copy-done | bytes 88
  9.3 0.0 copy-start.7
  9.4 0.7 %copy-done.7 = s32[4,4]{1,0:T(4,128)S(1)} copy-done((s32[4,4]{1,0:T(4,128)S(1)}, s32[4,4]{1,0:T(4,128)}, u32[]{:S(2)}) %copy-start.7) | copy-done | bytes 88
  10.0 0.0 copy-start.8
  10.0 0.7 %copy-done.8 = bf16[4,4]{1,0:T(4,128)(2,1)S(1)} copy-done((bf16[4,4]{1,0:T(4,128)(2,1)S(1)}, bf16[4,4]{1,0:T(4,128)(2,1)}, u32[]{:S(2)}) %copy-start.8) | copy-done | bytes 56
  10.7 0.7 %copy-done.9 = s32[4]{0:T(128)S(1)} copy-done((s32[4]{0:T(128)S(1)}, s32[4]{0:T(128)}, u32[]{:S(2)}) %copy-start.9) | copy-done | bytes 40
  11.4 51.0 %shard_map.148 = (bf16[4,192]{1,0:T(4,128)(2,1)S(1)}, bf16[4,128,128]{2,1,0:T(8,128)(2,1)S(1)}, bf16[4,128,128]{2,1,0:T(8,128)(2,1)S(1)}) custom-call(s32[4,4]{1,0:T(4,128)S(1)} %copy-done.6, s32[4]{0:T(128)S(1)} %copy-done.9, s32[1]{0:T(128)S(6)} %copy.19.leave_ref, s32[1]{0:T(128)S(6)} %copy.20.target_ref, bf16[4,320]{1,0:T(4,128)(2,1)S(1)} %copy-done.5, ...), custom_call_target="tpu_custom_call" | custom-call | tf_op jit(solution)/shard_map/pallas_call | solution.py:332
  62.4 0.6 copy.21
  63.0 0.7 %copy.22 = bf16[4,128,128]{2,1,0:T(8,128)(2,1)} copy(bf16[4,128,128]{2,1,0:T(8,128)(2,1)S(1)} %get-tuple-element.7) | data formatting | bytes 262144
  63.6 0.7 %copy.23 = bf16[4,128,128]{2,1,0:T(8,128)(2,1)} copy(bf16[4,128,128]{2,1,0:T(8,128)(2,1)S(1)} %get-tuple-element.8) | data formatting | bytes 262144
  (1 shorter events, 0.0 us)
Async XLA Ops:
  2.6 1.4 %copy-start = (bf16[1,1536,512]{2,1,0:T(8,128)(2,1)S(1)}, bf16[1,1536,512]{2,1,0:T(8,128)(2,1)}, u32[]{:S(2)}) copy-start(bf16[1,1536,512]{2,1,0:T(8,128)(2,1)} %win_hbm.1) | copy-start | bytes 4718596
  4.0 1.1 %copy-start.1 = (bf16[1,256,1536]{2,1,0:T(8,128)(2,1)S(1)}, bf16[1,256,1536]{2,1,0:T(8,128)(2,1)}, u32[]{:S(2)}) copy-start(bf16[1,256,1536]{2,1,0:T(8,128)(2,1)} %wd_hbm.1) | copy-start | bytes 2359300
  5.2 1.1 %copy-start.2 = (bf16[192,1536]{1,0:T(8,128)(2,1)S(1)}, bf16[192,1536]{1,0:T(8,128)(2,1)}, u32[]{:S(2)}) copy-start(bf16[192,1536]{1,0:T(8,128)(2,1)} %wo_hbm.1) | copy-start | bytes 1769476
  6.2 1.0 %copy-start.3 = (bf16[16,128,128]{2,1,0:T(8,128)(2,1)S(1)}, bf16[16,128,128]{2,1,0:T(8,128)(2,1)}, u32[]{:S(2)}) copy-start(bf16[16,128,128]{2,1,0:T(8,128)(2,1)} %pool_hbm.1) | copy-start | bytes 1572868
  7.3 0.7 %copy-start.4 = (bf16[4,1536]{1,0:T(4,128)(2,1)S(1)}, bf16[4,1536]{1,0:T(4,128)(2,1)}, u32[]{:S(2)}) copy-start(bf16[4,1536]{1,0:T(4,128)(2,1)} %res_ref.1) | copy-start | bytes 36868
  8.0 0.7 %copy-start.5 = (bf16[4,320]{1,0:T(4,128)(2,1)S(1)}, bf16[4,320]{1,0:T(4,128)(2,1)}, u32[]{:S(2)}) copy-start(bf16[4,320]{1,0:T(4,128)(2,1)} %qkv_ref.1) | copy-start | bytes 7684
  8.7 0.7 %copy-start.6 = (s32[4,4]{1,0:T(4,128)S(1)}, s32[4,4]{1,0:T(4,128)}, u32[]{:S(2)}) copy-start(s32[4,4]{1,0:T(4,128)} %pt_ref.1) | copy-start | bytes 196
  9.3 0.7 %copy-start.7 = (s32[4,4]{1,0:T(4,128)S(1)}, s32[4,4]{1,0:T(4,128)}, u32[]{:S(2)}) copy-start(s32[4,4]{1,0:T(4,128)} %ids_ref.1) | copy-start | bytes 196
  10.0 0.7 %copy-start.8 = (bf16[4,4]{1,0:T(4,128)(2,1)S(1)}, bf16[4,4]{1,0:T(4,128)(2,1)}, u32[]{:S(2)}) copy-start(bf16[4,4]{1,0:T(4,128)(2,1)} %gate_ref.1) | copy-start | bytes 100
  10.7 0.7 %copy-start.9 = (s32[4]{0:T(128)S(1)}, s32[4]{0:T(128)}, u32[]{:S(2)}) copy-start(s32[4]{0:T(128)} %len_ref.1) | copy-start | bytes 52

commit v2 on v1

--- a/solution.py
+++ b/solution.py
@@ -29,6 +29,22 @@
     nz,
     ny,
     ntp,
+    pt_hbm,
+    len_hbm,
+    leave_hbm,
+    target_hbm,
+    qkv_hbm,
+    res_hbm,
+    ids_hbm,
+    gate_hbm,
+    gain_hbm,
+    pool_hbm,
+    wo_hbm,
+    win_hbm,
+    wd_hbm,
+    hid_out,
+    newp_out,
+    arr_out,
     pt_ref,
     len_ref,
     leave_ref,
@@ -38,13 +54,6 @@
     ids_ref,
     gate_ref,
     gain_ref,
-    pool_hbm,
-    wo_hbm,
-    win_hbm,
-    wd_hbm,
-    hid_out,
-    newp_out,
-    arr_out,
     pool,
     wo,
     win,
@@ -67,6 +76,7 @@
     load_sem,
     send_sem,
     recv_sem,
+    ready_sem,
 ):
     rep = lax.axis_index("rep")
     tp = lax.axis_index("tp")
@@ -82,21 +92,45 @@
     def on_tp(step):
         return {"tp": lax.rem(tp + step, ntp)}
 
+    pairs = (
+        (pt_hbm, pt_ref),
+        (len_hbm, len_ref),
+        (leave_hbm, leave_ref),
+        (target_hbm, target_ref),
+        (qkv_hbm, qkv_ref),
+        (pool_hbm, pool),
+        (wo_hbm, wo),
+        (res_hbm, res_ref),
+        (ids_hbm, ids_ref),
+        (gate_hbm, gate_ref),
+        (gain_hbm, gain_ref),
+        (win_hbm.at[0], win),
+        (wd_hbm.at[0], wd),
+    )
     loads = [
-        pltpu.make_async_copy(pool_hbm, pool, load_sem.at[0]),
-        pltpu.make_async_copy(wo_hbm, wo, load_sem.at[1]),
-        pltpu.make_async_copy(win_hbm.at[0], win, load_sem.at[2]),
-        pltpu.make_async_copy(wd_hbm.at[0], wd, load_sem.at[3]),
+        pltpu.make_async_copy(src, dst, load_sem.at[i]) for i, (src, dst) in enumerate(pairs)
     ]
     for copy in loads:
         copy.start()
 
+    is_late = rep * ntp + tp == 0
+    late_y = jnp.logical_and(z * ntp + tp == 0, y != 0)
+    late_z = jnp.logical_and(y * ntp + tp == 0, z != 0)
+    late_tp = jnp.logical_and(rep == 0, tp != 0)
+    late_peer = jnp.logical_or(jnp.logical_or(late_y, late_z), late_tp)
+    everyone = [
+        peer(step)
+        for peer, count in ((on_y, ny), (on_z, nz), (on_tp, ntp))
+        for step in range(1, count)
+    ]
     barrier = pltpu.get_barrier_semaphore()
-    for peer, count in ((on_y, ny), (on_z, nz), (on_tp, ntp)):
-        for step in range(1, count):
-            pl.semaphore_signal(barrier, inc=1, device_id=peer(step), device_id_type=MESH)
-
-    def push(kind, step, src, dst, peer):
+
+    @pl.when(jnp.logical_not(is_late))
+    def _():
+        for device in everyone:
+            pl.semaphore_signal(barrier, inc=1, device_id=device, device_id_type=MESH)
+
+    def push(kind, step, src, dst, peer, start=None):
         copy = pltpu.make_async_remote_copy(
             src_ref=src,
             dst_ref=dst,
@@ -105,9 +139,14 @@
             device_id=peer(step),
             device_id_type=MESH,
         )
-        copy.start()
+        if start is None:
+            copy.start()
+        else:
+            pl.when(start)(copy.start)
         return copy
 
+    for copy in loads[0:5]:
+        copy.wait()
     leave = leave_ref[0]
     target = target_ref[0]
     low = lax.broadcasted_iota(jnp.int32, (8, LANES), 1) < HD
@@ -125,7 +164,7 @@
     ).astype(BF16)
     fresh = jnp.where(low, pltpu.roll(qkv_b, HD, 1), pltpu.roll(qkv_c, HD, 1))
 
-    loads[0].wait()
+    loads[5].wait()
     row_in_page = lax.broadcasted_iota(jnp.int32, (PAGE, LANES), 0)
     for r in range(REQ):
         new_row = fresh[r : r + 1, :]
@@ -140,9 +179,24 @@
             buf[0, i * PG : (i + 1) * PG] = cache[leave, p0 + i].reshape(PG, TILE, LANES)
         buf[0, 2 * PG] = header
 
-    pl.semaphore_wait(barrier, ny - 1 + nz - 1 + ntp - 1)
-    gather_a = [push(0, d, first_a.at[0], first_a.at[d], on_y) for d in range(1, ny)]
-    gather_b = [push(1, d, first_b.at[0], first_b.at[d], on_z) for d in range(1, nz)]
+    pl.semaphore_wait(barrier, len(everyone) - late_peer.astype(jnp.int32))
+
+    @pl.when(is_late)
+    def _():
+        for device in everyone:
+            pl.semaphore_signal(ready_sem, inc=1, device_id=device, device_id_type=MESH)
+
+    def not_late(flag, place, step, count):
+        return jnp.logical_not(jnp.logical_and(flag, place + step == count))
+
+    gather_a = [
+        push(0, d, first_a.at[0], first_a.at[d], on_y, not_late(late_y, y, d, ny))
+        for d in range(1, ny)
+    ]
+    gather_b = [
+        push(1, d, first_b.at[0], first_b.at[d], on_z, not_late(late_z, z, d, nz))
+        for d in range(1, nz)
+    ]
 
     span = MAXP * PAGE
     row_req = lax.broadcasted_iota(jnp.int32, (GROUP * 8, span), 0) & 7
@@ -165,11 +219,26 @@
         attn = attn + dot(jnp.where(row_req == r, probs, 0.0).astype(BF16), rows)
     heads01 = jnp.where(low, pltpu.roll(attn[0:8], HD, 1), attn[8:16]).astype(BF16)
     head2 = pltpu.roll(attn[16:24], HD, 1)[:, 0:HD].astype(BF16)
-    loads[1].wait()
+    loads[6].wait()
     part = dot(heads01, wo[0:LANES, :]) + dot(head2, wo[LANES : LANES + HD, :])
     parts[0] = part[0:REQ]
+
+    @pl.when(late_peer)
+    def _():
+        pl.semaphore_wait(ready_sem, 1)
+
+    @pl.when(late_y)
+    def _():
+        push(0, ny - y, first_a.at[0], first_a.at[ny - y], on_y)
+
+    @pl.when(late_z)
+    def _():
+        push(1, nz - z, first_b.at[0], first_b.at[nz - z], on_z)
+
     sum_heads = [push(2, d, parts.at[0], parts.at[d], on_tp) for d in range(1, ntp)]
 
+    for copy in loads[7:11]:
+        copy.wait()
     share = jnp.sum(
         jnp.where(ids_ref[...] == tp, gate_ref[...].astype(F32), 0.0), axis=1, keepdims=True
     )
@@ -181,13 +250,13 @@
     stream8[0:REQ, :] = total
     stream = stream8[...]
     mean_sq = jnp.mean(stream * stream, axis=1, keepdims=True)
-    normed = (stream * lax.rsqrt(mean_sq + 1e-05) * gain_ref[...]).astype(BF16)
-    loads[2].wait()
+    normed = (stream * lax.rsqrt(mean_sq + 1e-05) * gain_ref[...][None, :]).astype(BF16)
+    loads[11].wait()
     up = dot(normed, win[...])
     half = up.shape[1] // 2
     gate, lift = up[:, 0:half], up[:, half:]
     acted = (gate * (1.0 / (1.0 + jnp.exp(-gate))) * lift).astype(BF16)
-    loads[3].wait()
+    loads[12].wait()
     down = dot(acted, wd[...])
     stream8[0:REQ, :] = down[0:REQ] * share + jnp.where(tp == 0, 1.0, 0.0) * total
     cols = stream8.shape[1] // ntp
@@ -237,7 +306,6 @@
         return z * ny + lax.rem(y + e, ny)
 
     scatter_a = forward(first_a, send_a, last_a, gather_a, 4, on_z, nz, number_z)
-    scatter_b = forward(first_b, send_b, last_b, gather_b, 5, on_y, ny, number_y)
 
     hidden = share_out[tp]
     for d in range(1, ntp):
@@ -252,6 +320,7 @@
         jnp.where(row8 == 1, target, jnp.where(row8 == 2, page_no, 0)).astype(F32),
     )
     rows_y = [push(6, d, row_y.at[0], row_y.at[d], on_y) for d in range(1, ny)]
+    scatter_b = forward(first_b, send_b, last_b, gather_b, 5, on_y, ny, number_y)
     for copy in rows_y:
         copy.wait_recv()
     rows_z = []
@@ -303,6 +372,17 @@
     ):
         for copy in copies:
             copy.wait_send()
+
+
+def write_out(hid, newp, arr, hid_hbm, newp_hbm, arr_hbm, sem):
+    copies = [
+        pltpu.make_async_copy(src, dst, sem.at[i])
+        for i, (src, dst) in enumerate(((hid, hid_hbm), (newp, newp_hbm), (arr, arr_hbm)))
+    ]
+    for copy in copies:
+        copy.start()
+    for copy in copies:
+        copy.wait()
 
 
 def local(
@@ -326,19 +406,24 @@
     width = residual_in.shape[1]
     cols = width // ntp
     most = max(nz, ny, ntp)
-    smem = pl.BlockSpec(memory_space=pltpu.SMEM)
     vmem = pl.BlockSpec(memory_space=pltpu.VMEM)
-    hbm = pl.BlockSpec(memory_space=pl.ANY)
-    return pl.pallas_call(
+    hbm = pl.BlockSpec(memory_space=pltpu.HBM)
+    shapes = ((REQ, cols), (REQ, PAGE, LANES), (MAXP, PAGE, LANES))
+    results = pl.pallas_call(
         functools.partial(kernel, nz, ny, ntp),
-        out_shape=(
-            jax.ShapeDtypeStruct((REQ, cols), BF16),
-            jax.ShapeDtypeStruct((REQ, PAGE, LANES), BF16),
-            jax.ShapeDtypeStruct((MAXP, PAGE, LANES), BF16),
-        ),
-        in_specs=[smem] * 4 + [vmem] * 5 + [hbm] * 4,
+        out_shape=tuple(pltpu.VMEM(s, BF16) for s in shapes),
+        in_specs=[hbm] * 13,
         out_specs=(vmem, vmem, vmem),
         scratch_shapes=[
+            pltpu.SMEM(page_table.shape, jnp.int32),
+            pltpu.SMEM(req_lengths.shape, jnp.int32),
+            pltpu.SMEM(leave_slot.shape, jnp.int32),
+            pltpu.SMEM(target_rep.shape, jnp.int32),
+            pltpu.VMEM(qkv_new.shape, BF16),
+            pltpu.VMEM(residual_in.shape, BF16),
+            pltpu.VMEM(expert_ids.shape, jnp.int32),
+            pltpu.VMEM(gate_weights.shape, BF16),
+            pltpu.VMEM(norm_gain.shape, F32),
             pltpu.VMEM(kv_pool.shape, BF16),
             pltpu.VMEM(out_proj.shape, BF16),
             pltpu.VMEM(expert_in.shape[1:], BF16),
@@ -358,12 +443,13 @@
             pltpu.VMEM((ny, 8, 2 * LANES), F32),
             pltpu.VMEM((nz, 8, 2 * LANES), F32),
             pltpu.VMEM((nz, 8, 2 * LANES), F32),
-            pltpu.SemaphoreType.DMA((4,)),
+            pltpu.SemaphoreType.DMA((13,)),
             pltpu.SemaphoreType.DMA((8, most)),
             pltpu.SemaphoreType.DMA((8, most)),
+            pltpu.SemaphoreType.REGULAR,
         ],
         compiler_params=pltpu.CompilerParams(
-            collective_id=0, has_side_effects=True, vmem_limit_bytes=32 << 20
+            collective_id=0, has_side_effects=True, vmem_limit_bytes=60 << 20
         ),
     )(
         page_table,
@@ -374,12 +460,20 @@
         residual_in,
         expert_ids,
         gate_weights,
-        norm_gain[None, :],
+        norm_gain,
         kv_pool,
         out_proj,
         expert_in,
         expert_down,
     )
+    return pl.pallas_call(
+        write_out,
+        out_shape=tuple(jax.ShapeDtypeStruct(s, BF16) for s in shapes),
+        in_specs=[vmem] * 3,
+        out_specs=[hbm] * 3,
+        scratch_shapes=[pltpu.SemaphoreType.DMA((3,))],
+        compiler_params=pltpu.CompilerParams(vmem_limit_bytes=1 << 20),
+    )(*results)
 
 
 def solution(mesh):

time: 64.8 us -> 49.7 us (0.77)
  the two profiles are of different devices: /device:TPU:2 before, /device:TPU:1 now
where the time goes in v2:
time: 49.7 us; the launch traced here: 49.6 us
  Pallas kernels  47.6 us (96%)
  between operations  1.93 us (4%)
    pallas_call x1, Pallas kernels, local(): pl.pallas_call(functools.partial(kernel, nz, ny, ntp), out_shape=tuple((p...  46.9 us

profile of v2, /device:TPU:1, one launch (start us, length us, event | category | flops | bytes accessed | tf_op | source)
XLA Modules:
  0.0 49.6 jit_solution(3583632372684412018)
XLA Ops:
  1.9 46.9 %shard_map.148 = (bf16[4,192]{1,0:T(4,128)(2,1)S(1)}, bf16[4,128,128]{2,1,0:T(8,128)(2,1)S(1)}, bf16[4,128,128]{2,1,0:T(8,128)(2,1)S(1)}) custom-call(s32[4,4]{1,0:T(4,128)} %pt_hbm.1, s32[4]{0:T(128)} %len_hbm.1, s32[1]{0:T(128)S(6)} %copy.16.leave_hbm, s32[1]{0:T(128)S(6)} %copy.17.target_hbm, bf16[4,320]{1,0:T(4,128)(2,1)} %qkv_hbm.1, ...), custom_call_target="tpu_custom_call" | custom-call | tf_op jit(solution)/shard_map/pallas_call | solution.py:412
  48.8 0.7 %shard_map.149 = (bf16[4,192]{1,0:T(4,128)(2,1)}, bf16[4,128,128]{2,1,0:T(8,128)(2,1)}, bf16[4,128,128]{2,1,0:T(8,128)(2,1)}) custom-call(bf16[4,192]{1,0:T(4,128)(2,1)S(1)} %get-tuple-element.6.hid, bf16[4,128,128]{2,1,0:T(8,128)(2,1)S(1)} %get-tuple-element.7.newp, bf16[4,128,128]{2,1,0:T(8,128)(2,1)S(1)} %get-tuple-element.8.arr), custom_call_target="tpu_custom_call" | custom-call | tf_op jit(solution)/shard_map/pallas_call | solution.py:469

commit v3 on v2

--- a/solution.py
+++ b/solution.py
@@ -66,6 +66,8 @@
     send_b,
     last_a,
     last_b,
+    hops_a,
+    hops_b,
     parts,
     stream8,
     share_out,
@@ -130,13 +132,13 @@
         for device in everyone:
             pl.semaphore_signal(barrier, inc=1, device_id=device, device_id_type=MESH)
 
-    def push(kind, step, src, dst, peer, start=None):
+    def push(kind, sem, src, dst, device, start=None):
         copy = pltpu.make_async_remote_copy(
             src_ref=src,
             dst_ref=dst,
-            send_sem=send_sem.at[kind, step],
-            recv_sem=recv_sem.at[kind, step],
-            device_id=peer(step),
+            send_sem=send_sem.at[kind, sem],
+            recv_sem=recv_sem.at[kind, sem],
+            device_id=device,
             device_id_type=MESH,
         )
         if start is None:
@@ -175,9 +177,9 @@
 
     header = jnp.full((TILE, LANES), target, jnp.int32).astype(F32).astype(BF16)
     for buf, p0 in ((first_a, 0), (first_b, 2)):
-        for i in range(2):
-            buf[0, i * PG : (i + 1) * PG] = cache[leave, p0 + i].reshape(PG, TILE, LANES)
-        buf[0, 2 * PG] = header
+        buf[0, 0:PG] = cache[leave, p0].reshape(PG, TILE, LANES)
+        buf[0, PG] = header
+        buf[0, PG + 1 :] = cache[leave, p0 + 1].reshape(PG, TILE, LANES)
 
     pl.semaphore_wait(barrier, len(everyone) - late_peer.astype(jnp.int32))
 
@@ -186,17 +188,36 @@
         for device in everyone:
             pl.semaphore_signal(ready_sem, inc=1, device_id=device, device_id_type=MESH)
 
-    def not_late(flag, place, step, count):
-        return jnp.logical_not(jnp.logical_and(flag, place + step == count))
-
-    gather_a = [
-        push(0, d, first_a.at[0], first_a.at[d], on_y, not_late(late_y, y, d, ny))
-        for d in range(1, ny)
-    ]
-    gather_b = [
-        push(1, d, first_b.at[0], first_b.at[d], on_z, not_late(late_z, z, d, nz))
-        for d in range(1, nz)
-    ]
+    def to_late(flag, place, step, count):
+        return jnp.logical_and(flag, place + step == count)
+
+    def spread(kind, first, peer, flag, place, count):
+        near = {}
+        for d in (1, 2, count - 2, count - 1):
+            late = to_late(flag, place, d, count)
+            near[d] = push(kind, d, first.at[0], first.at[d], peer(d), jnp.logical_not(late))
+        return near
+
+    def spread_late(near, flag, place, count):
+        for d, copy in near.items():
+            pl.when(to_late(flag, place, d, count))(copy.start)
+
+    def pass_on(kind, first, peer, near):
+        upper, lower = pl.ds(0, PG + 1), pl.ds(PG + 1, PG)
+        near[2].wait_recv()
+        far = [
+            push(kind, 4, first.at[2, upper], first.at[4, upper], peer(2)),
+            push(kind, 3, first.at[2], first.at[3], peer(1)),
+        ]
+        near[6].wait_recv()
+        far += [
+            push(kind, 0, first.at[6, lower], first.at[4, lower], peer(6)),
+            push(kind, 5, first.at[6], first.at[5], peer(7)),
+        ]
+        return far
+
+    near_a = spread(0, first_a, on_y, late_y, y, ny)
+    near_b = spread(1, first_b, on_z, late_z, z, nz)
 
     span = MAXP * PAGE
     row_req = lax.broadcasted_iota(jnp.int32, (GROUP * 8, span), 0) & 7
@@ -227,15 +248,12 @@
     def _():
         pl.semaphore_wait(ready_sem, 1)
 
-    @pl.when(late_y)
-    def _():
-        push(0, ny - y, first_a.at[0], first_a.at[ny - y], on_y)
-
-    @pl.when(late_z)
-    def _():
-        push(1, nz - z, first_b.at[0], first_b.at[nz - z], on_z)
-
-    sum_heads = [push(2, d, parts.at[0], parts.at[d], on_tp) for d in range(1, ntp)]
+    spread_late(near_a, late_y, y, ny)
+    spread_late(near_b, late_z, z, nz)
+    sum_heads = [push(2, d, parts.at[0], parts.at[d], on_tp(d)) for d in range(1, ntp)]
+
+    far_a = pass_on(0, first_a, on_y, near_a)
+    far_b = pass_on(1, first_b, on_z, near_b)
 
     for copy in loads[7:11]:
         copy.wait()
@@ -277,27 +295,59 @@
             )
         share_out[t] = window
     sum_experts = [
-        push(3, d, share_out.at[lax.rem(tp + d, ntp)], share_in.at[d], on_tp)
+        push(3, d, share_out.at[lax.rem(tp + d, ntp)], share_in.at[d], on_tp(d))
         for d in range(1, ntp)
     ]
 
-    def forward(first, send, last, waits, kind, peer, count, number_of):
-        for copy in waits:
+    def scatter(first, near, far, send, last, hops, kind, peer, number_of):
+        near[1].wait_recv()
+        near[7].wait_recv()
+        for copy in far:
             copy.wait_recv()
-        heads = [first[d, 2 * PG].astype(F32) for d in range(len(waits) + 1)]
-        sent = []
-        for e in range(count):
+        heads = [first[d, PG].astype(F32) for d in range(8)]
+
+        def packet(e, out):
             wanted = number_of(e).astype(F32)
-            packet = jnp.zeros((2 * PG, TILE, LANES), BF16)
+            upper = jnp.zeros((PG, TILE, LANES), BF16)
+            lower = upper
             for d, head in enumerate(heads):
-                mine = jnp.where(head == wanted, 1.0, 0.0).astype(BF16)
-                packet = packet + first[d, 0 : 2 * PG] * mine[None]
-            if e == 0:
-                last[0] = packet
-            else:
-                send[e] = packet
-                sent.append(push(kind, e, send.at[e], last.at[e], peer))
+                mine = jnp.where(head == wanted, 1.0, 0.0).astype(BF16)[None]
+                upper = upper + first[d, 0:PG] * mine
+                lower = lower + first[d, PG + 1 :] * mine
+            out[0:PG] = upper
+            out[PG:] = lower
+
+        def send_to(e, sem, src, dst):
+            return push(kind, sem, src, dst, peer(e))
+
+        packet(4, send.at[4])
+        sent = {
+            4: send_to(2, 4, send.at[4, pl.ds(0, PG)], hops.at[2, pl.ds(0, PG)]),
+            0: send_to(6, 0, send.at[4, pl.ds(PG, PG)], hops.at[2, pl.ds(PG, PG)]),
+        }
+        packet(3, send.at[3])
+        sent[3] = send_to(1, 3, send.at[3], hops.at[0])
+        packet(5, send.at[5])
+        sent[5] = send_to(7, 5, send.at[5], hops.at[1])
+        for e in (1, 7):
+            packet(e, send.at[e])
+            sent[e] = send_to(e, e, send.at[e], last.at[e])
+        for e in (2, 6):
+            packet(e, send.at[e])
+        packet(0, last.at[0])
         return sent
+
+    def scatter_on(sent, send, last, hops, kind, peer):
+        sent[3].wait_recv()
+        sent[4].wait_recv()
+        send[2] = send[2] + hops[0]
+        send[2, 0:PG] = send[2, 0:PG] + hops[2, 0:PG]
+        sent[2] = push(kind, 2, send.at[2], last.at[2], peer(2))
+        sent[5].wait_recv()
+        sent[0].wait_recv()
+        send[6] = send[6] + hops[1]
+        send[6, PG:] = send[6, PG:] + hops[2, PG:]
+        sent[6] = push(kind, 6, send.at[6], last.at[6], peer(6))
 
     def number_z(e):
         return lax.rem(z + e, nz) * ny + y
@@ -305,7 +355,7 @@
     def number_y(e):
         return z * ny + lax.rem(y + e, ny)
 
-    scatter_a = forward(first_a, send_a, last_a, gather_a, 4, on_z, nz, number_z)
+    sent_a = scatter(first_a, near_a, far_a, send_a, last_a, hops_a, 4, on_z, number_z)
 
     hidden = share_out[tp]
     for d in range(1, ntp):
@@ -319,8 +369,10 @@
         leaving,
         jnp.where(row8 == 1, target, jnp.where(row8 == 2, page_no, 0)).astype(F32),
     )
-    rows_y = [push(6, d, row_y.at[0], row_y.at[d], on_y) for d in range(1, ny)]
-    scatter_b = forward(first_b, send_b, last_b, gather_b, 5, on_y, ny, number_y)
+    rows_y = [push(6, d, row_y.at[0], row_y.at[d], on_y(d)) for d in range(1, ny)]
+    sent_b = scatter(first_b, near_b, far_b, send_b, last_b, hops_b, 5, on_y, number_y)
+    scatter_on(sent_a, send_a, last_a, hops_a, 4, on_z)
+    scatter_on(sent_b, send_b, last_b, hops_b, 5, on_y)
     for copy in rows_y:
         copy.wait_recv()
     rows_z = []
@@ -334,7 +386,7 @@
             row_z[0] = message
         else:
             row_send[e] = message
-            rows_z.append(push(7, e, row_send.at[e], row_z.at[e], on_z))
+            rows_z.append(push(7, e, row_send.at[e], row_z.at[e], on_z(e)))
     message = row_z[0]
     for e in range(1, nz):
         rows_z[e - 1].wait_recv()
@@ -344,10 +396,10 @@
 
     came_page = jnp.broadcast_to(message[2:3, 0:LANES], (TILE, LANES))
     moved = jnp.zeros((PG, TILE, LANES), BF16)
-    for last, waits, p0 in ((last_a, scatter_a, 0), (last_b, scatter_b, 2)):
+    for last, sent, p0 in ((last_a, sent_a, 0), (last_b, sent_b, 2)):
         came = last[0]
-        for e in range(1, len(waits) + 1):
-            waits[e - 1].wait_recv()
+        for e in (1, 7, 2, 6):
+            sent[e].wait_recv()
             came = came + last[e]
         for i in range(2):
             page = came[i * PG : (i + 1) * PG]
@@ -361,12 +413,14 @@
         newp_out[r] = page.reshape(PAGE, LANES)
 
     for copies in (
-        gather_a,
-        gather_b,
+        near_a.values(),
+        near_b.values(),
+        far_a,
+        far_b,
         sum_heads,
         sum_experts,
-        scatter_a,
-        scatter_b,
+        sent_a.values(),
+        sent_b.values(),
         rows_y,
         rows_z,
     ):
@@ -436,6 +490,8 @@
             pltpu.VMEM((ny, 2 * PG, TILE, LANES), BF16),
             pltpu.VMEM((nz, 2 * PG, TILE, LANES), BF16),
             pltpu.VMEM((ny, 2 * PG, TILE, LANES), BF16),
+            pltpu.VMEM((3, 2 * PG, TILE, LANES), BF16),
+            pltpu.VMEM((3, 2 * PG, TILE, LANES), BF16),
             pltpu.VMEM((ntp, REQ, width), F32),
             pltpu.VMEM((8, width), F32),
             pltpu.VMEM((ntp, 8, 2 * LANES), F32),

time: 49.7 us -> 41.5 us (0.84)
  the two profiles are of different devices: /device:TPU:1 before, /device:TPU:2 now
where the time goes in v3:
time: 41.5 us; the launch traced here: 41.4 us
  Pallas kernels  39.4 us (95%)
  between operations  1.93 us (5%)
    pallas_call x1, Pallas kernels, local(): pl.pallas_call(functools.partial(kernel, nz, ny, ntp), out_shape=tuple((p...  38.7 us

profile of v3, /device:TPU:2, one launch (start us, length us, event | category | flops | bytes accessed | tf_op | source)
XLA Modules:
  0.0 41.4 jit_solution(17615445384682706454)
XLA Ops:
  1.9 38.7 %shard_map.148 = (bf16[4,192]{1,0:T(4,128)(2,1)S(1)}, bf16[4,128,128]{2,1,0:T(8,128)(2,1)S(1)}, bf16[4,128,128]{2,1,0:T(8,128)(2,1)S(1)}) custom-call(s32[4,4]{1,0:T(4,128)} %pt_hbm.1, s32[4]{0:T(128)} %len_hbm.1, s32[1]{0:T(128)S(6)} %copy.16.leave_hbm, s32[1]{0:T(128)S(6)} %copy.17.target_hbm, bf16[4,320]{1,0:T(4,128)(2,1)} %qkv_hbm.1, ...), custom_call_target="tpu_custom_call" | custom-call | tf_op jit(solution)/shard_map/pallas_call | solution.py:466
  40.6 0.7 %shard_map.149 = (bf16[4,192]{1,0:T(4,128)(2,1)}, bf16[4,128,128]{2,1,0:T(8,128)(2,1)}, bf16[4,128,128]{2,1,0:T(8,128)(2,1)}) custom-call(bf16[4,192]{1,0:T(4,128)(2,1)S(1)} %get-tuple-element.6.hid, bf16[4,128,128]{2,1,0:T(8,128)(2,1)S(1)} %get-tuple-element.7.newp, bf16[4,128,128]{2,1,0:T(8,128)(2,1)S(1)} %get-tuple-element.8.arr), custom_call_target="tpu_custom_call" | custom-call | tf_op jit(solution)/shard_map/pallas_call | solution.py:525

commit v4 on v3

--- a/solution.py
+++ b/solution.py
@@ -59,6 +59,7 @@
     win,
     wd,
     qs,
+    new_kv,
     cache,
     first_a,
     first_b,
@@ -112,18 +113,25 @@
     loads = [
         pltpu.make_async_copy(src, dst, load_sem.at[i]) for i, (src, dst) in enumerate(pairs)
     ]
-    for copy in loads:
+    for copy in loads[0:6]:
         copy.start()
 
     is_late = rep * ntp + tp == 0
-    late_y = jnp.logical_and(z * ntp + tp == 0, y != 0)
-    late_z = jnp.logical_and(y * ntp + tp == 0, z != 0)
+    near_y = (1, 2, ny - 2, ny - 1)
+    near_z = (1, 2, nz - 2, nz - 1)
+
+    def beside(place, steps):
+        hits = [place == step for step in steps]
+        return functools.reduce(jnp.logical_or, hits)
+
+    late_y = jnp.logical_and(z * ntp + tp == 0, beside(y, near_y))
+    late_z = jnp.logical_and(y * ntp + tp == 0, beside(z, near_z))
     late_tp = jnp.logical_and(rep == 0, tp != 0)
     late_peer = jnp.logical_or(jnp.logical_or(late_y, late_z), late_tp)
     everyone = [
         peer(step)
-        for peer, count in ((on_y, ny), (on_z, nz), (on_tp, ntp))
-        for step in range(1, count)
+        for peer, steps in ((on_y, near_y), (on_z, near_z), (on_tp, range(1, ntp)))
+        for step in steps
     ]
     barrier = pltpu.get_barrier_semaphore()
 
@@ -131,6 +139,12 @@
     def _():
         for device in everyone:
             pl.semaphore_signal(barrier, inc=1, device_id=device, device_id_type=MESH)
+
+    @pl.when(is_late)
+    def _():
+        pl.semaphore_wait(barrier, len(everyone))
+        for device in everyone:
+            pl.semaphore_signal(ready_sem, inc=1, device_id=device, device_id_type=MESH)
 
     def push(kind, sem, src, dst, device, start=None):
         copy = pltpu.make_async_remote_copy(
@@ -167,33 +181,32 @@
     fresh = jnp.where(low, pltpu.roll(qkv_b, HD, 1), pltpu.roll(qkv_c, HD, 1))
 
     loads[5].wait()
+    for copy in loads[6:]:
+        copy.start()
+    new_kv[...] = fresh
     row_in_page = lax.broadcasted_iota(jnp.int32, (PAGE, LANES), 0)
-    for r in range(REQ):
-        new_row = fresh[r : r + 1, :]
-        for p in range(MAXP):
-            page = pool[pt_ref[r, p]].astype(F32)
-            at_token = row_in_page == len_ref[r] - p * PAGE
-            cache[r, p] = jnp.where(at_token, new_row, page).astype(BF16)
+
+    def with_token(r, p):
+        at_token = row_in_page == len_ref[r] - p * PAGE
+        page = pool[pt_ref[r, p]].astype(F32)
+        return jnp.where(at_token, new_kv[pl.ds(r, 1), :], page).astype(BF16)
 
     header = jnp.full((TILE, LANES), target, jnp.int32).astype(F32).astype(BF16)
     for buf, p0 in ((first_a, 0), (first_b, 2)):
-        buf[0, 0:PG] = cache[leave, p0].reshape(PG, TILE, LANES)
+        buf[0, 0:PG] = with_token(leave, p0).reshape(PG, TILE, LANES)
         buf[0, PG] = header
-        buf[0, PG + 1 :] = cache[leave, p0 + 1].reshape(PG, TILE, LANES)
-
-    pl.semaphore_wait(barrier, len(everyone) - late_peer.astype(jnp.int32))
-
-    @pl.when(is_late)
+        buf[0, PG + 1 :] = with_token(leave, p0 + 1).reshape(PG, TILE, LANES)
+
+    @pl.when(jnp.logical_not(is_late))
     def _():
-        for device in everyone:
-            pl.semaphore_signal(ready_sem, inc=1, device_id=device, device_id_type=MESH)
+        pl.semaphore_wait(barrier, len(everyone) - late_peer.astype(jnp.int32))
 
     def to_late(flag, place, step, count):
         return jnp.logical_and(flag, place + step == count)
 
     def spread(kind, first, peer, flag, place, count):
         near = {}
-        for d in (1, 2, count - 2, count - 1):
+        for d in (2, count - 2, 1, count - 1):
             late = to_late(flag, place, d, count)
             near[d] = push(kind, d, first.at[0], first.at[d], peer(d), jnp.logical_not(late))
         return near
@@ -218,6 +231,10 @@
 
     near_a = spread(0, first_a, on_y, late_y, y, ny)
     near_b = spread(1, first_b, on_z, late_z, z, nz)
+
+    for r in range(REQ):
+        for p in range(MAXP):
+            cache[r, p] = with_token(r, p)
 
     span = MAXP * PAGE
     row_req = lax.broadcasted_iota(jnp.int32, (GROUP * 8, span), 0) & 7
@@ -242,7 +259,7 @@
     head2 = pltpu.roll(attn[16:24], HD, 1)[:, 0:HD].astype(BF16)
     loads[6].wait()
     part = dot(heads01, wo[0:LANES, :]) + dot(head2, wo[LANES : LANES + HD, :])
-    parts[0] = part[0:REQ]
+    parts[0] = part[0:REQ].astype(BF16)
 
     @pl.when(late_peer)
     def _():
@@ -260,10 +277,10 @@
     share = jnp.sum(
         jnp.where(ids_ref[...] == tp, gate_ref[...].astype(F32), 0.0), axis=1, keepdims=True
     )
-    total = res_ref[...].astype(F32) + parts[0]
+    total = res_ref[...].astype(F32) + part[0:REQ]
     for d in range(1, ntp):
         sum_heads[d - 1].wait_recv()
-        total = total + parts[d]
+        total = total + parts[d].astype(F32)
     stream8[...] = jnp.zeros_like(stream8)
     stream8[0:REQ, :] = total
     stream = stream8[...]
@@ -293,7 +310,7 @@
                 ],
                 axis=1,
             )
-        share_out[t] = window
+        share_out[t] = window[0:REQ]
     sum_experts = [
         push(3, d, share_out.at[lax.rem(tp + d, ntp)], share_in.at[d], on_tp(d))
         for d in range(1, ntp)
@@ -361,13 +378,18 @@
     for d in range(1, ntp):
         sum_experts[d - 1].wait_recv()
         hidden = hidden + share_in[d]
-    row8 = lax.broadcasted_iota(jnp.int32, hidden.shape, 0)
-    leaving = jnp.sum(jnp.where(row8 == leave, hidden, 0.0), axis=0, keepdims=True)
+    slot_no = lax.broadcasted_iota(jnp.int32, hidden.shape, 0)
+    leaving = jnp.sum(jnp.where(slot_no == leave, hidden, 0.0), axis=0, keepdims=True)
     page_no = lax.shift_right_logical(len_ref[leave], 7)
+    line = lax.broadcasted_iota(jnp.int32, (4, LANES), 0)
     row_y[0] = jnp.where(
-        row8 == 0,
-        leaving,
-        jnp.where(row8 == 1, target, jnp.where(row8 == 2, page_no, 0)).astype(F32),
+        line == 0,
+        leaving[:, 0:LANES],
+        jnp.where(
+            line == 1,
+            leaving[:, LANES:],
+            jnp.where(line == 2, target, page_no).astype(F32),
+        ),
     )
     rows_y = [push(6, d, row_y.at[0], row_y.at[d], on_y(d)) for d in range(1, ny)]
     sent_b = scatter(first_b, near_b, far_b, send_b, last_b, hops_b, 5, on_y, number_y)
@@ -378,10 +400,10 @@
     rows_z = []
     for e in range(nz):
         wanted = number_z(e).astype(F32)
-        message = jnp.zeros(hidden.shape, F32)
+        message = jnp.zeros((4, LANES), F32)
         for d in range(ny):
             one = row_y[d]
-            message = message + jnp.where(one[1:2, :] == wanted, 1.0, 0.0) * one
+            message = message + jnp.where(one[2:3, :] == wanted, 1.0, 0.0) * one
         if e == 0:
             row_z[0] = message
         else:
@@ -391,10 +413,11 @@
     for e in range(1, nz):
         rows_z[e - 1].wait_recv()
         message = message + row_z[e]
-    hidden = jnp.where(row8 == leave, message[0:1, :], hidden)
+    moved_row = jnp.concatenate([message[0:1, :], message[1:2, :]], axis=1)
+    hidden = jnp.where(slot_no == leave, moved_row, hidden)
     hid_out[...] = hidden[0:REQ, 0:cols].astype(BF16)
 
-    came_page = jnp.broadcast_to(message[2:3, 0:LANES], (TILE, LANES))
+    came_page = jnp.broadcast_to(message[3:4, :], (TILE, LANES))
     moved = jnp.zeros((PG, TILE, LANES), BF16)
     for last, sent, p0 in ((last_a, sent_a, 0), (last_b, sent_b, 2)):
         came = last[0]
@@ -483,6 +506,7 @@
             pltpu.VMEM(expert_in.shape[1:], BF16),
             pltpu.VMEM(expert_down.shape[1:], BF16),
             pltpu.VMEM((8, 3 * LANES), F32),
+            pltpu.VMEM((8, LANES), F32),
             pltpu.VMEM((REQ, MAXP, PAGE, LANES), BF16),
             pltpu.VMEM((ny, 2 * PG + 1, TILE, LANES), BF16),
             pltpu.VMEM((nz, 2 * PG + 1, TILE, LANES), BF16),
@@ -492,13 +516,13 @@
             pltpu.VMEM((ny, 2 * PG, TILE, LANES), BF16),
             pltpu.VMEM((3, 2 * PG, TILE, LANES), BF16),
             pltpu.VMEM((3, 2 * PG, TILE, LANES), BF16),
-            pltpu.VMEM((ntp, REQ, width), F32),
+            pltpu.VMEM((ntp, REQ, width), BF16),
             pltpu.VMEM((8, width), F32),
-            pltpu.VMEM((ntp, 8, 2 * LANES), F32),
-            pltpu.VMEM((ntp, 8, 2 * LANES), F32),
-            pltpu.VMEM((ny, 8, 2 * LANES), F32),
-            pltpu.VMEM((nz, 8, 2 * LANES), F32),
-            pltpu.VMEM((nz, 8, 2 * LANES), F32),
+            pltpu.VMEM((ntp, REQ, 2 * LANES), F32),
+            pltpu.VMEM((ntp, REQ, 2 * LANES), F32),
+            pltpu.VMEM((ny, 4, LANES), F32),
+            pltpu.VMEM((nz, 4, LANES), F32),
+            pltpu.VMEM((nz, 4, LANES), F32),
             pltpu.SemaphoreType.DMA((13,)),
             pltpu.SemaphoreType.DMA((8, most)),
             pltpu.SemaphoreType.DMA((8, most)),

time: 41.5 us -> 39.1 us (0.942)
  the two profiles are of different devices: /device:TPU:2 before, /device:TPU:8 now
where the time goes in v4:
time: 39.1 us; the launch traced here: 39 us
  Pallas kernels  37 us (95%)
  between operations  1.93 us (5%)
    pallas_call x1, Pallas kernels, local(): pl.pallas_call(functools.partial(kernel, nz, ny, ntp), out_shape=tuple((p...  36.3 us

profile of v4, /device:TPU:8, one launch (start us, length us, event | category | flops | bytes accessed | tf_op | source)
XLA Modules:
  0.0 39.0 jit_solution(12975158507594594776)
XLA Ops:
  1.9 36.3 %shard_map.148 = (bf16[4,192]{1,0:T(4,128)(2,1)S(1)}, bf16[4,128,128]{2,1,0:T(8,128)(2,1)S(1)}, bf16[4,128,128]{2,1,0:T(8,128)(2,1)S(1)}) custom-call(s32[4,4]{1,0:T(4,128)} %pt_hbm.1, s32[4]{0:T(128)} %len_hbm.1, s32[1]{0:T(128)S(6)} %copy.16.leave_hbm, s32[1]{0:T(128)S(6)} %copy.17.target_hbm, bf16[4,320]{1,0:T(4,128)(2,1)} %qkv_hbm.1, ...), custom_call_target="tpu_custom_call" | custom-call | tf_op jit(solution)/shard_map/pallas_call | solution.py:489
  38.2 0.7 %shard_map.149 = (bf16[4,192]{1,0:T(4,128)(2,1)}, bf16[4,128,128]{2,1,0:T(8,128)(2,1)}, bf16[4,128,128]{2,1,0:T(8,128)(2,1)}) custom-call(bf16[4,192]{1,0:T(4,128)(2,1)S(1)} %get-tuple-element.6.hid, bf16[4,128,128]{2,1,0:T(8,128)(2,1)S(1)} %get-tuple-element.7.newp, bf16[4,128,128]{2,1,0:T(8,128)(2,1)S(1)} %get-tuple-element.8.arr), custom_call_target="tpu_custom_call" | custom-call | tf_op jit(solution)/shard_map/pallas_call | solution.py:549

commit v5 on v4

--- a/solution.py
+++ b/solution.py
@@ -86,14 +86,10 @@
     z = lax.div(rep, ny)
     y = lax.rem(rep, ny)
 
-    def on_y(step):
-        return {"rep": z * ny + lax.rem(y + step, ny)}
-
-    def on_z(step):
-        return {"rep": lax.rem(z + step, nz) * ny + y}
-
-    def on_tp(step):
-        return {"tp": lax.rem(tp + step, ntp)}
+    ring_y = [{"rep": z * ny + lax.rem(y + step, ny)} for step in range(ny)]
+    ring_z = [{"rep": lax.rem(z + step, nz) * ny + y} for step in range(nz)]
+    ring_tp = [{"tp": lax.rem(tp + step, ntp)} for step in range(ntp)]
+    on_y, on_z, on_tp = ring_y.__getitem__, ring_z.__getitem__, ring_tp.__getitem__
 
     pairs = (
         (pt_hbm, pt_ref),
@@ -259,7 +255,7 @@
     head2 = pltpu.roll(attn[16:24], HD, 1)[:, 0:HD].astype(BF16)
     loads[6].wait()
     part = dot(heads01, wo[0:LANES, :]) + dot(head2, wo[LANES : LANES + HD, :])
-    parts[0] = part[0:REQ].astype(BF16)
+    parts[0] = part[0:REQ]
 
     @pl.when(late_peer)
     def _():
@@ -280,7 +276,7 @@
     total = res_ref[...].astype(F32) + part[0:REQ]
     for d in range(1, ntp):
         sum_heads[d - 1].wait_recv()
-        total = total + parts[d].astype(F32)
+        total = total + parts[d]
     stream8[...] = jnp.zeros_like(stream8)
     stream8[0:REQ, :] = total
     stream = stream8[...]
@@ -349,10 +345,12 @@
         for e in (1, 7):
             packet(e, send.at[e])
             sent[e] = send_to(e, e, send.at[e], last.at[e])
-        for e in (2, 6):
-            packet(e, send.at[e])
-        packet(0, last.at[0])
-        return sent
+        def rest():
+            for e in (2, 6):
+                packet(e, send.at[e])
+            packet(0, last.at[0])
+
+        return sent, rest
 
     def scatter_on(sent, send, last, hops, kind, peer):
         sent[3].wait_recv()
@@ -367,12 +365,12 @@
         sent[6] = push(kind, 6, send.at[6], last.at[6], peer(6))
 
     def number_z(e):
-        return lax.rem(z + e, nz) * ny + y
+        return ring_z[e]["rep"]
 
     def number_y(e):
-        return z * ny + lax.rem(y + e, ny)
-
-    sent_a = scatter(first_a, near_a, far_a, send_a, last_a, hops_a, 4, on_z, number_z)
+        return ring_y[e]["rep"]
+
+    sent_a, rest_a = scatter(first_a, near_a, far_a, send_a, last_a, hops_a, 4, on_z, number_z)
 
     hidden = share_out[tp]
     for d in range(1, ntp):
@@ -392,9 +390,9 @@
         ),
     )
     rows_y = [push(6, d, row_y.at[0], row_y.at[d], on_y(d)) for d in range(1, ny)]
-    sent_b = scatter(first_b, near_b, far_b, send_b, last_b, hops_b, 5, on_y, number_y)
-    scatter_on(sent_a, send_a, last_a, hops_a, 4, on_z)
-    scatter_on(sent_b, send_b, last_b, hops_b, 5, on_y)
+    sent_b, rest_b = scatter(first_b, near_b, far_b, send_b, last_b, hops_b, 5, on_y, number_y)
+    rest_a()
+    rest_b()
     for copy in rows_y:
         copy.wait_recv()
     rows_z = []
@@ -409,6 +407,8 @@
         else:
             row_send[e] = message
             rows_z.append(push(7, e, row_send.at[e], row_z.at[e], on_z(e)))
+    scatter_on(sent_a, send_a, last_a, hops_a, 4, on_z)
+    scatter_on(sent_b, send_b, last_b, hops_b, 5, on_y)
     message = row_z[0]
     for e in range(1, nz):
         rows_z[e - 1].wait_recv()
@@ -516,7 +516,7 @@
             pltpu.VMEM((ny, 2 * PG, TILE, LANES), BF16),
             pltpu.VMEM((3, 2 * PG, TILE, LANES), BF16),
             pltpu.VMEM((3, 2 * PG, TILE, LANES), BF16),
-            pltpu.VMEM((ntp, REQ, width), BF16),
+            pltpu.VMEM((ntp, REQ, width), F32),
             pltpu.VMEM((8, width), F32),
             pltpu.VMEM((ntp, REQ, 2 * LANES), F32),
             pltpu.VMEM((ntp, REQ, 2 * LANES), F32),

time: 39.1 us -> 38.5 us (0.985)
  the two profiles are of different devices: /device:TPU:8 before, /device:TPU:1 now
where the time goes in v5:
time: 38.5 us; the launch traced here: 38.1 us
  Pallas kernels  36.2 us (94%)
  between operations  1.93 us (5%)
    pallas_call x1, Pallas kernels, local(): pl.pallas_call(functools.partial(kernel, nz, ny, ntp), out_shape=tuple((p...  35.4 us

profile of v5, /device:TPU:1, one launch (start us, length us, event | category | flops | bytes accessed | tf_op | source)
XLA Modules:
  0.0 38.1 jit_solution(4870005823096398983)
XLA Ops:
  1.9 35.4 %shard_map.148 = (bf16[4,192]{1,0:T(4,128)(2,1)S(1)}, bf16[4,128,128]{2,1,0:T(8,128)(2,1)S(1)}, bf16[4,128,128]{2,1,0:T(8,128)(2,1)S(1)}) custom-call(s32[4,4]{1,0:T(4,128)} %pt_hbm.1, s32[4]{0:T(128)} %len_hbm.1, s32[1]{0:T(128)S(6)} %copy.16.leave_hbm, s32[1]{0:T(128)S(6)} %copy.17.target_hbm, bf16[4,320]{1,0:T(4,128)(2,1)} %qkv_hbm.1, ...), custom_call_target="tpu_custom_call" | custom-call | tf_op jit(solution)/shard_map/pallas_call | solution.py:489
  37.4 0.7 %shard_map.149 = (bf16[4,192]{1,0:T(4,128)(2,1)}, bf16[4,128,128]{2,1,0:T(8,128)(2,1)}, bf16[4,128,128]{2,1,0:T(8,128)(2,1)}) custom-call(bf16[4,192]{1,0:T(4,128)(2,1)S(1)} %get-tuple-element.6.hid, bf16[4,128,128]{2,1,0:T(8,128)(2,1)S(1)} %get-tuple-element.7.newp, bf16[4,128,128]{2,1,0:T(8,128)(2,1)S(1)} %get-tuple-element.8.arr), custom_call_target="tpu_custom_call" | custom-call | tf_op jit(solution)/shard_map/pallas_call | solution.py:549

commit v6 on v4

--- a/solution.py
+++ b/solution.py
@@ -192,10 +192,11 @@
         return jnp.where(at_token, new_kv[pl.ds(r, 1), :], page).astype(BF16)
 
     header = jnp.full((TILE, LANES), target, jnp.int32).astype(F32).astype(BF16)
-    for buf, p0 in ((first_a, 0), (first_b, 2)):
-        buf[0, 0:PG] = with_token(leave, p0).reshape(PG, TILE, LANES)
-        buf[0, PG] = header
-        buf[0, PG + 1 :] = with_token(leave, p0 + 1).reshape(PG, TILE, LANES)
+    for c in range(2):
+        for buf, p0 in ((first_a, 0), (first_b, 2)):
+            buf[c, 0, 0:PG] = with_token(leave, p0 + c).reshape(PG, TILE, LANES)
+            if c == 0:
+                buf[0, 0, PG] = header
 
     @pl.when(jnp.logical_not(is_late))
     def _():
@@ -204,33 +205,35 @@
     def to_late(flag, place, step, count):
         return jnp.logical_and(flag, place + step == count)
 
-    def spread(kind, first, peer, flag, place, count):
+    def slot(first, c, d):
+        return first.at[c, d] if c == 0 else first.at[c, d, pl.ds(0, PG)]
+
+    def spread(kind, first, c, peer, flag, place, count):
         near = {}
-        for d in (2, count - 2, 1, count - 1):
+        for d in (2, 6, 1, 7):
             late = to_late(flag, place, d, count)
-            near[d] = push(kind, d, first.at[0], first.at[d], peer(d), jnp.logical_not(late))
+            near[d] = push(
+                kind, d, slot(first, c, 0), slot(first, c, d), peer(d), jnp.logical_not(late)
+            )
         return near
 
     def spread_late(near, flag, place, count):
         for d, copy in near.items():
             pl.when(to_late(flag, place, d, count))(copy.start)
 
-    def pass_on(kind, first, peer, near):
-        upper, lower = pl.ds(0, PG + 1), pl.ds(PG + 1, PG)
-        near[2].wait_recv()
-        far = [
-            push(kind, 4, first.at[2, upper], first.at[4, upper], peer(2)),
-            push(kind, 3, first.at[2], first.at[3], peer(1)),
-        ]
-        near[6].wait_recv()
-        far += [
-            push(kind, 0, first.at[6, lower], first.at[4, lower], peer(6)),
-            push(kind, 5, first.at[6], first.at[5], peer(7)),
-        ]
+    def pass_on(kind, first, c, peer, near):
+        far = []
+        for held, d, step in ((2, 3, 1), (6, 5, 7)):
+            near[held].wait_recv()
+            if held == (2, 6)[c]:
+                far.append(push(kind, 4, slot(first, c, held), slot(first, c, 4), peer(held)))
+            far.append(push(kind, d, slot(first, c, held), slot(first, c, d), peer(step)))
         return far
 
-    near_a = spread(0, first_a, on_y, late_y, y, ny)
-    near_b = spread(1, first_b, on_z, late_z, z, nz)
+    near_a, near_b = [], []
+    for c in range(2):
+        near_a.append(spread(c, first_a, c, on_y, late_y, y, ny))
+        near_b.append(spread(2 + c, first_b, c, on_z, late_z, z, nz))
 
     for r in range(REQ):
         for p in range(MAXP):
@@ -259,18 +262,21 @@
     head2 = pltpu.roll(attn[16:24], HD, 1)[:, 0:HD].astype(BF16)
     loads[6].wait()
     part = dot(heads01, wo[0:LANES, :]) + dot(head2, wo[LANES : LANES + HD, :])
-    parts[0] = part[0:REQ].astype(BF16)
+    parts[0] = part[0:REQ]
 
     @pl.when(late_peer)
     def _():
         pl.semaphore_wait(ready_sem, 1)
 
-    spread_late(near_a, late_y, y, ny)
-    spread_late(near_b, late_z, z, nz)
-    sum_heads = [push(2, d, parts.at[0], parts.at[d], on_tp(d)) for d in range(1, ntp)]
-
-    far_a = pass_on(0, first_a, on_y, near_a)
-    far_b = pass_on(1, first_b, on_z, near_b)
+    for c in range(2):
+        spread_late(near_a[c], late_y, y, ny)
+        spread_late(near_b[c], late_z, z, nz)
+    sum_heads = [push(8, d, parts.at[0], parts.at[d], on_tp(d)) for d in range(1, ntp)]
+
+    far_a, far_b = [], []
+    for c in range(2):
+        far_a.append(pass_on(c, first_a, c, on_y, near_a[c]))
+        far_b.append(pass_on(2 + c, first_b, c, on_z, near_b[c]))
 
     for copy in loads[7:11]:
         copy.wait()
@@ -280,7 +286,7 @@
     total = res_ref[...].astype(F32) + part[0:REQ]
     for d in range(1, ntp):
         sum_heads[d - 1].wait_recv()
-        total = total + parts[d].astype(F32)
+        total = total + parts[d]
     stream8[...] = jnp.zeros_like(stream8)
     stream8[0:REQ, :] = total
     stream = stream8[...]
@@ -312,59 +318,50 @@
             )
         share_out[t] = window[0:REQ]
     sum_experts = [
-        push(3, d, share_out.at[lax.rem(tp + d, ntp)], share_in.at[d], on_tp(d))
+        push(9, d, share_out.at[lax.rem(tp + d, ntp)], share_in.at[d], on_tp(d))
         for d in range(1, ntp)
     ]
 
-    def scatter(first, near, far, send, last, hops, kind, peer, number_of):
+    def scatter(first, c, near, far, send, last, hops, kind, peer, number_of):
         near[1].wait_recv()
         near[7].wait_recv()
         for copy in far:
             copy.wait_recv()
-        heads = [first[d, PG].astype(F32) for d in range(8)]
+        heads = [first[0, d, PG].astype(F32) for d in range(8)]
 
         def packet(e, out):
             wanted = number_of(e).astype(F32)
-            upper = jnp.zeros((PG, TILE, LANES), BF16)
-            lower = upper
+            total = jnp.zeros((PG, TILE, LANES), BF16)
             for d, head in enumerate(heads):
                 mine = jnp.where(head == wanted, 1.0, 0.0).astype(BF16)[None]
-                upper = upper + first[d, 0:PG] * mine
-                lower = lower + first[d, PG + 1 :] * mine
-            out[0:PG] = upper
-            out[PG:] = lower
-
-        def send_to(e, sem, src, dst):
-            return push(kind, sem, src, dst, peer(e))
-
-        packet(4, send.at[4])
-        sent = {
-            4: send_to(2, 4, send.at[4, pl.ds(0, PG)], hops.at[2, pl.ds(0, PG)]),
-            0: send_to(6, 0, send.at[4, pl.ds(PG, PG)], hops.at[2, pl.ds(PG, PG)]),
-        }
-        packet(3, send.at[3])
-        sent[3] = send_to(1, 3, send.at[3], hops.at[0])
-        packet(5, send.at[5])
-        sent[5] = send_to(7, 5, send.at[5], hops.at[1])
-        for e in (1, 7):
-            packet(e, send.at[e])
-            sent[e] = send_to(e, e, send.at[e], last.at[e])
+                total = total + first[c, d, 0:PG] * mine
+            out[...] = total
+
+        sent = {}
+        over = (2, 6)[c]
+        for e, step, out in (
+            (4, over, hops.at[c, 2]),
+            (3, 1, hops.at[c, 0]),
+            (5, 7, hops.at[c, 1]),
+            (1, 1, last.at[c, 1]),
+            (7, 7, last.at[c, 7]),
+        ):
+            packet(e, send.at[c, e])
+            sent[e] = push(kind, e, send.at[c, e], out, peer(step))
         for e in (2, 6):
-            packet(e, send.at[e])
-        packet(0, last.at[0])
+            packet(e, send.at[c, e])
+        packet(0, last.at[c, 0])
         return sent
 
-    def scatter_on(sent, send, last, hops, kind, peer):
-        sent[3].wait_recv()
-        sent[4].wait_recv()
-        send[2] = send[2] + hops[0]
-        send[2, 0:PG] = send[2, 0:PG] + hops[2, 0:PG]
-        sent[2] = push(kind, 2, send.at[2], last.at[2], peer(2))
-        sent[5].wait_recv()
-        sent[0].wait_recv()
-        send[6] = send[6] + hops[1]
-        send[6, PG:] = send[6, PG:] + hops[2, PG:]
-        sent[6] = push(kind, 6, send.at[6], last.at[6], peer(6))
+    def scatter_on(sent, c, send, last, hops, kind, peer):
+        for e, came, hop in ((2, 3, 0), (6, 5, 1)):
+            sent[came].wait_recv()
+            total = send[c, e] + hops[c, hop]
+            if e == (2, 6)[c]:
+                sent[4].wait_recv()
+                total = total + hops[c, 2]
+            send[c, e] = total
+            sent[e] = push(kind, e, send.at[c, e], last.at[c, e], peer(e))
 
     def number_z(e):
         return lax.rem(z + e, nz) * ny + y
@@ -372,7 +369,17 @@
     def number_y(e):
         return z * ny + lax.rem(y + e, ny)
 
-    sent_a = scatter(first_a, near_a, far_a, send_a, last_a, hops_a, 4, on_z, number_z)
+    sent_a, sent_b = [], []
+
+    def scatter_a(c):
+        args = (first_a, c, near_a[c], far_a[c], send_a, last_a, hops_a)
+        sent_a.append(scatter(*args, 4 + c, on_z, number_z))
+
+    def scatter_b(c):
+        args = (first_b, c, near_b[c], far_b[c], send_b, last_b, hops_b)
+        sent_b.append(scatter(*args, 6 + c, on_y, number_y))
+
+    scatter_a(0)
 
     hidden = share_out[tp]
     for d in range(1, ntp):
@@ -391,10 +398,10 @@
             jnp.where(line == 2, target, page_no).astype(F32),
         ),
     )
-    rows_y = [push(6, d, row_y.at[0], row_y.at[d], on_y(d)) for d in range(1, ny)]
-    sent_b = scatter(first_b, near_b, far_b, send_b, last_b, hops_b, 5, on_y, number_y)
-    scatter_on(sent_a, send_a, last_a, hops_a, 4, on_z)
-    scatter_on(sent_b, send_b, last_b, hops_b, 5, on_y)
+    rows_y = [push(10, d, row_y.at[0], row_y.at[d], on_y(d)) for d in range(1, ny)]
+    scatter_b(0)
+    scatter_a(1)
+    scatter_b(1)
     for copy in rows_y:
         copy.wait_recv()
     rows_z = []
@@ -408,7 +415,11 @@
             row_z[0] = message
         else:
             row_send[e] = message
-            rows_z.append(push(7, e, row_send.at[e], row_z.at[e], on_z(e)))
+            rows_z.append(push(11, e, row_send.at[e], row_z.at[e], on_z(e)))
+    scatter_on(sent_a[0], 0, send_a, last_a, hops_a, 4, on_z)
+    scatter_on(sent_b[0], 0, send_b, last_b, hops_b, 6, on_y)
+    scatter_on(sent_a[1], 1, send_a, last_a, hops_a, 5, on_z)
+    scatter_on(sent_b[1], 1, send_b, last_b, hops_b, 7, on_y)
     message = row_z[0]
     for e in range(1, nz):
         rows_z[e - 1].wait_recv()
@@ -419,15 +430,14 @@
 
     came_page = jnp.broadcast_to(message[3:4, :], (TILE, LANES))
     moved = jnp.zeros((PG, TILE, LANES), BF16)
-    for last, sent, p0 in ((last_a, sent_a, 0), (last_b, sent_b, 2)):
-        came = last[0]
-        for e in (1, 7, 2, 6):
-            sent[e].wait_recv()
-            came = came + last[e]
-        for i in range(2):
-            page = came[i * PG : (i + 1) * PG]
-            arr_out[p0 + i] = page.reshape(PAGE, LANES)
-            mine = jnp.where(came_page == float(p0 + i), 1.0, 0.0).astype(BF16)
+    for c in range(2):
+        for last, sent, p0 in ((last_a, sent_a, 0), (last_b, sent_b, 2)):
+            page = last[c, 0]
+            for e in (1, 7, 2, 6):
+                sent[c][e].wait_recv()
+                page = page + last[c, e]
+            arr_out[p0 + c] = page.reshape(PAGE, LANES)
+            mine = jnp.where(came_page == float(p0 + c), 1.0, 0.0).astype(BF16)
             moved = moved + page * mine[None]
     for r in range(REQ):
         kept = jnp.full((TILE, LANES), jnp.where(leave == r, 0.0, 1.0), F32)
@@ -436,14 +446,12 @@
         newp_out[r] = page.reshape(PAGE, LANES)
 
     for copies in (
-        near_a.values(),
-        near_b.values(),
-        far_a,
-        far_b,
+        *(near.values() for near in near_a + near_b),
+        *far_a,
+        *far_b,
         sum_heads,
         sum_experts,
-        sent_a.values(),
-        sent_b.values(),
+        *(sent.values() for sent in sent_a + sent_b),
         rows_y,
         rows_z,
     ):
@@ -508,15 +516,15 @@
             pltpu.VMEM((8, 3 * LANES), F32),
             pltpu.VMEM((8, LANES), F32),
             pltpu.VMEM((REQ, MAXP, PAGE, LANES), BF16),
-            pltpu.VMEM((ny, 2 * PG + 1, TILE, LANES), BF16),
-            pltpu.VMEM((nz, 2 * PG + 1, TILE, LANES), BF16),
-            pltpu.VMEM((nz, 2 * PG, TILE, LANES), BF16),
-            pltpu.VMEM((ny, 2 * PG, TILE, LANES), BF16),
-            pltpu.VMEM((nz, 2 * PG, TILE, LANES), BF16),
-            pltpu.VMEM((ny, 2 * PG, TILE, LANES), BF16),
-            pltpu.VMEM((3, 2 * PG, TILE, LANES), BF16),
-            pltpu.VMEM((3, 2 * PG, TILE, LANES), BF16),
-            pltpu.VMEM((ntp, REQ, width), BF16),
+            pltpu.VMEM((2, ny, PG + 1, TILE, LANES), BF16),
+            pltpu.VMEM((2, nz, PG + 1, TILE, LANES), BF16),
+            pltpu.VMEM((2, nz, PG, TILE, LANES), BF16),
+            pltpu.VMEM((2, ny, PG, TILE, LANES), BF16),
+            pltpu.VMEM((2, nz, PG, TILE, LANES), BF16),
+            pltpu.VMEM((2, ny, PG, TILE, LANES), BF16),
+            pltpu.VMEM((2, 3, PG, TILE, LANES), BF16),
+            pltpu.VMEM((2, 3, PG, TILE, LANES), BF16),
+            pltpu.VMEM((ntp, REQ, width), F32),
             pltpu.VMEM((8, width), F32),
             pltpu.VMEM((ntp, REQ, 2 * LANES), F32),
             pltpu.VMEM((ntp, REQ, 2 * LANES), F32),
@@ -524,8 +532,8 @@
             pltpu.VMEM((nz, 4, LANES), F32),
             pltpu.VMEM((nz, 4, LANES), F32),
             pltpu.SemaphoreType.DMA((13,)),
-            pltpu.SemaphoreType.DMA((8, most)),
-            pltpu.SemaphoreType.DMA((8, most)),
+            pltpu.SemaphoreType.DMA((12, most)),
+            pltpu.SemaphoreType.DMA((12, most)),
             pltpu.SemaphoreType.REGULAR,
         ],
         compiler_params=pltpu.CompilerParams(

time: 39.1 us -> 40.2 us (1.028)
  the two profiles are of different devices: /device:TPU:8 before, /device:TPU:1 now
where the time goes in v6:
time: 40.2 us; the launch traced here: 40.1 us
  Pallas kernels  38.1 us (95%)
  between operations  1.93 us (5%)
    pallas_call x1, Pallas kernels, local(): pl.pallas_call(functools.partial(kernel, nz, ny, ntp), out_shape=tuple((p...  37.4 us

profile of v6, /device:TPU:1, one launch (start us, length us, event | category | flops | bytes accessed | tf_op | source)
XLA Modules:
  0.0 40.1 jit_solution(5478376376811906883)
XLA Ops:
  1.9 37.4 %shard_map.148 = (bf16[4,192]{1,0:T(4,128)(2,1)S(1)}, bf16[4,128,128]{2,1,0:T(8,128)(2,1)S(1)}, bf16[4,128,128]{2,1,0:T(8,128)(2,1)S(1)}) custom-call(s32[4,4]{1,0:T(4,128)} %pt_hbm.1, s32[4]{0:T(128)} %len_hbm.1, s32[1]{0:T(128)S(6)} %copy.16.leave_hbm, s32[1]{0:T(128)S(6)} %copy.17.target_hbm, bf16[4,320]{1,0:T(4,128)(2,1)} %qkv_hbm.1, ...), custom_call_target="tpu_custom_call" | custom-call | tf_op jit(solution)/shard_map/pallas_call | solution.py:497
  39.3 0.7 %shard_map.149 = (bf16[4,192]{1,0:T(4,128)(2,1)}, bf16[4,128,128]{2,1,0:T(8,128)(2,1)}, bf16[4,128,128]{2,1,0:T(8,128)(2,1)}) custom-call(bf16[4,192]{1,0:T(4,128)(2,1)S(1)} %get-tuple-element.6.hid, bf16[4,128,128]{2,1,0:T(8,128)(2,1)S(1)} %get-tuple-element.7.newp, bf16[4,128,128]{2,1,0:T(8,128)(2,1)S(1)} %get-tuple-element.8.arr), custom_call_target="tpu_custom_call" | custom-call | tf_op jit(solution)/shard_map/pallas_call | solution.py:557
